TPU v7x, 128 devices: a whole 4x4x4 slice. The times are simulated.
128 devices in a mesh: gx: 4 (over z), gy: 4 (over x), gz: 8 (over y, core).
Axes of the slice: x: 4, y: 4, z: 4, core: 2. Of those that a mesh axis runs over, the one named last changes fastest.
Arguments:
- cotangent: float32 [19, 32, 64, 1024], P(None, 'gx', 'gy', 'gz'), may hold values from -6 to 6
- densities: float32 [3, 32, 64, 1024], P(None, 'gx', 'gy', 'gz'), may hold values from 0.3 to 2.2
- velocities: float32 [3, 3, 32, 64, 1024], P(None, None, 'gx', 'gy', 'gz'), may hold values from -0.16 to 0.16
- adhesion: float32 [32, 64, 1024], P('gx', 'gy', 'gz'), may hold values from -1 to 1
- fluid: int32 [32, 64, 1024], P('gx', 'gy', 'gz'), may hold values 0 or 1
Outputs:
- initial_cotangent: float32 [19, 32, 64, 1024], P(None, 'gx', 'gy', 'gz')
- adhesion_grad: float32 [32, 64, 1024], P('gx', 'gy', 'gz')
All inputs are finite; a program needn't handle non-finite values. No bound on the sum of `fluid` on one device may be relied on, other than what follows from the above.
Results may differ from a plain program's by a relative error of at most 0.00002.
Values sent between devices are 32-bit elements; how exact they have to be, the bound alone decides.
A program may use at most 64 MiB of HBM per device.

v0:
```python
import functools
import itertools

import jax
import jax.numpy as jnp
from jax import lax
from jax.experimental import pallas as pl
from jax.experimental.pallas import tpu as pltpu
from jax.sharding import PartitionSpec as P

DIRECTIONS = (
    (0, 0, 0), (1, 0, 0), (-1, 0, 0), (0, 1, 0), (0, -1, 0), (0, 0, 1), (0, 0, -1),
    (1, 1, 0), (-1, -1, 0), (1, -1, 0), (-1, 1, 0),
    (1, 0, 1), (-1, 0, -1), (1, 0, -1), (-1, 0, 1),
    (0, 1, 1), (0, -1, -1), (0, 1, -1), (0, -1, 1),
)
W0, W1, W2 = 1.0 / 3.0, 1.0 / 18.0, 1.0 / 36.0
TAU = 0.8
G = -5.0
STEPS = 3
NX, NY, NZ = 8, 16, 128
MESH = pl.DeviceIdType.MESH

SLOTS = (
    (1, -1, 0), (1, 0, 0), (1, 0, 1), (1, 0, -1), (1, 1, 0),
    (0, 1, 0), (0, 1, 1), (0, 1, -1),
    (-1, 1, 0), (-1, 0, 0), (-1, 0, -1), (-1, 0, 1), (-1, -1, 0),
    (0, -1, 0), (0, -1, -1), (0, -1, 1),
    None,
    (0, 0, 1), (0, 0, -1), (0, 0, 0),
)
SLOT = {c: k for k, c in enumerate(SLOTS) if c is not None}
COPY = 16
ZPOP = (
    ((0, 0, 1), (1, 0, 1), (-1, 0, 1), (0, 1, 1), (0, -1, 1)),
    ((0, 0, -1), (1, 0, -1), (-1, 0, -1), (0, 1, -1), (0, -1, -1)),
)
PAIRS = tuple((c, tuple(-t for t in c)) for c in DIRECTIONS[1::2])
NEIGHBOURS = (
    [(dx, 0, 0) for dx in (-1, 1)]
    + [(dx, dy, 0) for dx in (-1, 1) for dy in (-1, 1)]
    + [(dx, 0, dz) for dx in (-1, 1) for dz in (-1, 1)]
    + [(0, dy, dz) for dy in (-1, 1) for dz in (-1, 1)]
    + [(0, dy, 0) for dy in (-1, 1)]
    + [(0, 0, dz) for dz in (-1, 1)]
)
OWN = pl.ds(8, NY)


def position(field, x):
    return 2 + 10 * field + x


def rolled(values, shift):
    return pltpu.roll(values, shift, 1)


def kernel(sizes, cot, dens, vel, adh, flu, out, grad,
           cbuf, dbuf, ubuf, adbuf, fibuf, fbuf, abuf, vbuf, bbuf, mbuf, nbuf, obuf, gbuf,
           zs, zr, ze, hz, uz, send_sem, recv_sem, in_sem, out_sem):
    index = [lax.axis_index(a) for a in ("gx", "gy", "gz")]
    lane = lax.broadcasted_iota(jnp.int32, (NY, NZ), 1)
    first, last = lane == 0, lane == NZ - 1

    def present(d):
        found = None
        for axis in range(3):
            if d[axis] == 0:
                continue
            at = index[axis] + d[axis]
            inside = at >= 0 if d[axis] < 0 else at < sizes[axis]
            found = inside if found is None else jnp.logical_and(found, inside)
        return found

    def device(d):
        return tuple(index[axis] + d[axis] for axis in range(3))

    here = {d: present(d) for d in NEIGHBOURS}

    def message(kind, buf, n, d):
        dx, dy, dz = d
        if dz == 0:
            if kind == "a":
                if dx == 0:
                    slots = pl.ds(4, 5) if dy < 0 else pl.ds(12, 5)
                elif dy == 0:
                    slots = pl.ds(0, 5) if dx < 0 else pl.ds(8, 5)
                else:
                    slots = pl.ds(SLOT[(-dx, -dy, 0)], 1)
            else:
                slots = pl.ds(0, 4 if kind == "f" else 3)
            xs = (pl.ds(1, NX),) * 2 if dx == 0 else ((pl.ds(1, 1), pl.ds(9, 1)) if dx < 0 else (pl.ds(8, 1), pl.ds(0, 1)))
            ys = (OWN,) * 2 if dy == 0 else ((pl.ds(8, 1), pl.ds(24, 1)) if dy < 0 else (pl.ds(23, 1), pl.ds(7, 1)))
            return buf.at[xs[0], slots, ys[0]], buf.at[xs[1], slots, ys[1]]
        k = 0 if dz < 0 else 1
        if dx != 0:
            return zs.at[n, k], ze.at[n, k, 0 if dx < 0 else 1]
        if dy == 0:
            return zs.at[n, k], zr.at[n, k, OWN]
        ys = (pl.ds(0, 1), pl.ds(24, 1)) if dy < 0 else (pl.ds(15, 1), pl.ds(7, 1))
        return zs.at[n, k, ys[0]], zr.at[n, k, ys[1]]

    def copy(kind, buf, n, d, to):
        source, target = message(kind, buf, n, d)
        j = NEIGHBOURS.index(d)
        return pltpu.make_async_remote_copy(
            src_ref=source, dst_ref=target, send_sem=send_sem.at[n, j], recv_sem=recv_sem.at[n, j],
            device_id=device(to), device_id_type=MESH)

    def send(kind, buf, n):
        for d in NEIGHBOURS:
            @pl.when(here[d])
            def _():
                copy(kind, buf, n, d, d).start()

    def receive(kind, buf, n, fields):
        for d in NEIGHBOURS:
            source = tuple(-t for t in d)
            @pl.when(here[source])
            def _():
                copy(kind, buf, n, d, source).wait_recv()
        right = functools.reduce(jnp.logical_or, [lane == position(f, NX) for f in range(fields)])
        left = functools.reduce(jnp.logical_or, [lane == position(f, -1) for f in range(fields)])
        for k in range(2):
            face = zr[n, k, OWN, :]
            face = jnp.where(right, rolled(ze[n, k, 0], 8), face)
            face = jnp.where(left, rolled(ze[n, k, 1], NZ - 8), face)
            zr[n, k, OWN, :] = face

    def sent(kind, buf, n):
        for d in NEIGHBOURS:
            @pl.when(here[d])
            def _():
                copy(kind, buf, n, d, d).wait_send()

    def pack(faces, field, x, low, high):
        at = position(field, x)
        mine = lane == at
        zero, one = faces
        if low is not None:
            zero = jnp.where(mine, rolled(low, at), zero)
        if high is not None:
            one = jnp.where(mine, rolled(high, at + 1), one)
        return zero, one

    def moved(values, packed, field, x, cz):
        at = position(field, x)
        if cz > 0:
            return jnp.where(last, rolled(packed, NZ - 1 - at), rolled(values, NZ - 1))
        return jnp.where(first, rolled(packed, NZ - at), rolled(values, 1))

    barrier = pltpu.get_barrier_semaphore()
    for d in NEIGHBOURS:
        @pl.when(here[d])
        def _():
            pl.semaphore_signal(barrier, inc=1, device_id=device(d), device_id_type=MESH)
    loads = [
        pltpu.make_async_copy(source, target, in_sem.at[k])
        for k, (source, target) in enumerate(((flu, fibuf), (adh, adbuf), (dens, dbuf), (cot, cbuf), (vel, ubuf)))
    ]
    for load in loads:
        load.start()
    blank = jnp.zeros((NY, NZ), jnp.float32)
    row = jnp.zeros((1, NZ), jnp.float32)
    for e, d in enumerate(((1, 0, 0), (-1, 0, 0))):
        @pl.when(jnp.logical_not(here[d]))
        def _():
            p = NX + 1 if e == 0 else 0
            for f in range(4):
                fbuf[p, f, 0:16, :] = blank
                fbuf[p, f, 16:32, :] = blank
            for f in range(3):
                for s in range(STEPS):
                    vbuf[s, p, f, 0:16, :] = blank
                    vbuf[s, p, f, 16:32, :] = blank
            for n in (0, 2, 4, 6):
                for k in range(2):
                    ze[n, k, e] = blank
    for r, d in ((24, (0, 1, 0)), (7, (0, -1, 0))):
        @pl.when(jnp.logical_not(here[d]))
        def _():
            for p in range(NX + 2):
                for f in range(4):
                    fbuf[p, f, r:r + 1, :] = row
                for f in range(3):
                    for s in range(STEPS):
                        vbuf[s, p, f, r:r + 1, :] = row
            for n in (0, 2, 4, 6):
                for k in range(2):
                    zr[n, k, r:r + 1, :] = row
    for k, d in enumerate(((0, 0, 1), (0, 0, -1))):
        @pl.when(jnp.logical_not(here[d]))
        def _():
            for n in (0, 2, 4, 6):
                zr[n, k, 0:16, :] = blank
                zr[n, k, 16:32, :] = blank
                for e in range(2):
                    ze[n, k, e] = blank

    for k in range(3):
        loads[k].wait()

    def fixed(x, faces):
        fl = fibuf[x].astype(jnp.float32)
        wall = (1.0 - fl) * adbuf[x]
        fields = [fl]
        for s in range(STEPS):
            fields.append(fl * (G * (1.0 - jnp.exp(-dbuf[s, x]))) + wall)
        for f, value in enumerate(fields):
            fbuf[x + 1, f, OWN, :] = value
            faces = pack(faces, f, x, value, value)
        return faces

    faces = lax.fori_loop(0, NX, fixed, (blank, blank))
    zs[0, 0], zs[0, 1] = faces
    pl.semaphore_wait(barrier, sum(here[d].astype(jnp.int32) for d in NEIGHBOURS))
    send("f", fbuf, 0)

    loads[3].wait()

    def store_plane(buf, x, populations, faces):
        for c, value in populations.items():
            buf[x + 1, SLOT[c], OWN, :] = value
            if c == (1, -1, 0):
                buf[x + 1, COPY, 16:24, :] = value[8:16]
        for k in range(2):
            for j, c in enumerate(ZPOP[k]):
                value = populations[c]
                faces = pack(faces, j, x, value if k == 0 else None, value if k == 1 else None)
        return faces

    def masked(x, faces):
        fl = fbuf[x + 1, 0, OWN, :]
        return store_plane(abuf.at[STEPS - 1], x, {c: fl * cbuf[i, x] for i, c in enumerate(DIRECTIONS)}, faces)

    faces = lax.fori_loop(0, NX, masked, (blank, blank))
    zs[1, 0], zs[1, 1] = faces
    send("a", abuf.at[STEPS - 1], 1)

    receive("f", fbuf, 0, 4)
    for k in range(2):
        face = zr[0, k, OWN, :]
        up, down = zr[0, k, 9:25, :], zr[0, k, 7:23, :]
        ahead, behind = rolled(face, NZ - 1), rolled(face, 1)
        hz[k, 0] = ahead - behind
        hz[k, 1] = up - down
        hz[k, 2] = W1 * face + W2 * ((ahead + behind) + (up + down))

    def flags(x, carry):
        for i, c in enumerate(DIRECTIONS[1:]):
            cx, cy, cz = c
            beside = fbuf[x + 1 + cx, 0, 8 + cy:24 + cy, :]
            if cz != 0:
                k = 0 if cz > 0 else 1
                beside = moved(beside, zr[0, k, 8 + cy:24 + cy, :], 0, x + cx, cz)
            nbuf[x, i] = beside
        return carry

    lax.fori_loop(0, NX, flags, 0)
    loads[4].wait()

    def stream_plane(s, n, x, faces):
        a = abuf.at[s]
        b = {(0, 0, 0): a[x + 1, SLOT[(0, 0, 0)], OWN, :]}
        for c in DIRECTIONS[1:]:
            cx, cy, cz = c
            away = a[x + 1 + cx, SLOT[c], 8 + cy:24 + cy, :]
            if cz != 0:
                k = 0 if cz > 0 else 1
                away = moved(away, zr[n, k, 8 + cy:24 + cy, :], ZPOP[k].index(c), x + cx, cz)
            back = a[x + 1, SLOT[tuple(-t for t in c)], OWN, :]
            b[c] = jnp.where(nbuf[x, DIRECTIONS.index(c) - 1] != 0.0, away, back)
        for i, c in enumerate(DIRECTIONS):
            bbuf[x, i] = b[c]
        total = {}
        gap = {}
        for c, o in PAIRS:
            total[c] = b[c] + b[o]
            gap[c] = b[c] - b[o]
        w1, w2 = W1 / TAU, W2 / TAU
        sx, sy, sz = total[(1, 0, 0)], total[(0, 1, 0)], total[(0, 0, 1)]
        pxy, mxy = total[(1, 1, 0)], total[(1, -1, 0)]
        pxz, mxz = total[(1, 0, 1)], total[(1, 0, -1)]
        pyz, myz = total[(0, 1, 1)], total[(0, 1, -1)]
        txy, txz, tyz = pxy + mxy, pxz + mxz, pyz + myz
        m0 = (W0 / TAU) * b[(0, 0, 0)] + w1 * (sx + sy + sz) + w2 * (txy + txz + tyz)
        mxx = w1 * sx + w2 * (txy + txz)
        myy = w1 * sy + w2 * (txy + tyz)
        mzz = w1 * sz + w2 * (txz + tyz)
        hxy, hxz, hyz = w2 * (pxy - mxy), w2 * (pxz - mxz), w2 * (pyz - myz)
        dxp, dxm = gap[(1, 1, 0)], gap[(1, -1, 0)]
        ezp, ezm = gap[(1, 0, 1)], gap[(1, 0, -1)]
        fzp, fzm = gap[(0, 1, 1)], gap[(0, 1, -1)]
        m1x = w1 * gap[(1, 0, 0)] + w2 * ((dxp + dxm) + (ezp + ezm))
        m1y = w1 * gap[(0, 1, 0)] + w2 * ((dxp - dxm) + (fzp + fzm))
        m1z = w1 * gap[(0, 0, 1)] + w2 * ((ezp - ezm) + (fzp - fzm))
        ux, uy, uz_ = ubuf[s, 0, x], ubuf[s, 1, x], ubuf[s, 2, x]
        qx = mxx * ux + hxy * uy + hxz * uz_
        qy = hxy * ux + myy * uy + hyz * uz_
        qz = hxz * ux + hyz * uy + mzz * uz_
        speed = ux * ux + uy * uy + uz_ * uz_
        m3 = 3.0 * m0
        mbar = (3.0 * m1x + 9.0 * qx - ux * m3, 3.0 * m1y + 9.0 * qy - uy * m3, 3.0 * m1z + 9.0 * qz - uz_ * m3)
        mbuf[x, 0] = m0 + 1.5 * speed * m0 - 4.5 * (ux * qx + uy * qy + uz_ * qz)
        scale = fbuf[x + 1, 0, OWN, :] * (TAU * (1.0 - jnp.exp(-dbuf[s, x])))
        for k in range(3):
            mbuf[x, 1 + k] = mbar[k]
            value = scale * mbar[k]
            vbuf[s, x + 1, k, OWN, :] = value
            faces = pack(faces, k, x, value, value)
        return faces

    def force_plane(s, x, carry):
        f = 1 + s
        def phi(cx, cy):
            return fbuf[x + 1 + cx, f, 8 + cy:24 + cy, :]
        pp, pm, mp, mm = phi(1, 1), phi(1, -1), phi(-1, 1), phi(-1, -1)
        xp, xm, yp, ym = phi(1, 0), phi(-1, 0), phi(0, 1), phi(0, -1)
        dx, dy = xp - xm, yp - ym
        t = W1 * phi(0, 0) + W2 * ((xp + xm) + (yp + ym))
        def at(q, values, cz):
            return moved(values, hz[0 if cz > 0 else 1, q], f, x, cz)
        px = W1 * dx + W2 * ((pp - mp) + (pm - mm) + (at(0, dx, 1) + at(0, dx, -1)))
        py = W1 * dy + W2 * ((pp - pm) + (mp - mm) + (at(1, dy, 1) + at(1, dy, -1)))
        pz = at(2, t, 1) - at(2, t, -1)
        dot = mbuf[x, 1] * px + mbuf[x, 2] * py + mbuf[x, 3] * pz
        mbuf[x, 0] = mbuf[x, 0] - (TAU * jnp.exp(-dbuf[s, x])) * dot
        return carry

    def collide_plane(s, x, faces):
        v = vbuf.at[s]
        fl = fbuf[x + 1, 0, OWN, :]
        def at(k, cx, cy):
            return v[x + 1 + cx, k, 8 + cy:24 + cy, :]
        d = W2 * ((at(0, -1, 0) - at(0, 1, 0)) + (at(1, 0, -1) - at(1, 0, 1)))
        t = W1 * at(2, 0, 0) + W2 * ((at(2, -1, 0) + at(2, 1, 0)) + (at(2, 0, -1) + at(2, 0, 1)))
        gathered = 2.0 * d + W2 * (
            (at(0, -1, -1) + at(1, -1, -1)) - (at(0, 1, 1) + at(1, 1, 1))
            + (at(0, -1, 1) - at(1, -1, 1)) - (at(0, 1, -1) - at(1, 1, -1)))
        gathered = gathered + moved(d + t, uz[1], 0, x, -1) + moved(d - t, uz[0], 0, x, 1)
        part = (fl - 1.0) * gathered
        if s == STEPS - 1:
            gbuf[x] = part
        else:
            gbuf[x] = gbuf[x] + part
        density_bar = mbuf[x, 0] - (G * jnp.exp(-dbuf[s, x])) * (fl * gathered)
        mx, my, mz = mbuf[x, 1], mbuf[x, 2], mbuf[x, 3]
        sums = {(1, 0, 0): mx, (0, 1, 0): my, (0, 0, 1): mz,
                (1, 1, 0): mx + my, (1, -1, 0): mx - my, (1, 0, 1): mx + mz,
                (1, 0, -1): mx - mz, (0, 1, 1): my + mz, (0, 1, -1): my - mz}
        keep = 1.0 - 1.0 / TAU
        populations = {(0, 0, 0): fl * (keep * bbuf[x, 0] + density_bar)}
        for c, o in PAIRS:
            populations[c] = fl * (keep * bbuf[x, DIRECTIONS.index(c)] + (density_bar + sums[c]))
            populations[o] = fl * (keep * bbuf[x, DIRECTIONS.index(o)] + (density_bar - sums[c]))
        if s > 0:
            return store_plane(abuf.at[s - 1], x, populations, faces)
        for i, c in enumerate(DIRECTIONS):
            obuf[x, i] = populations[c]
        pltpu.make_async_copy(obuf.at[x], out.at[:, x], out_sem.at[x]).start()
        return faces

    for s in reversed(range(STEPS)):
        n = 1 + 2 * (STEPS - 1 - s)
        a, v = abuf.at[s], vbuf.at[s]
        receive("a", a, n, 5)
        for x in range(NX):
            a[x + 1, SLOT[(1, -1, 0)], 7:8, :] = a[x + 1, COPY, 7:8, :]
        faces = lax.fori_loop(0, NX, functools.partial(stream_plane, s, n), (blank, blank))
        zs[n + 1, 0], zs[n + 1, 1] = faces
        send("v", v, n + 1)
        lax.fori_loop(0, NX, functools.partial(force_plane, s), 0)
        receive("v", v, n + 1, 3)
        for k in range(2):
            face = zr[n + 1, k, OWN, :]
            up, down = zr[n + 1, k, 9:25, :], zr[n + 1, k, 7:23, :]
            ahead, behind = rolled(face, NZ - 1), rolled(face, 1)
            d = W2 * ((behind - ahead) + rolled(down - up, NZ - 10))
            t = rolled(W1 * face + W2 * ((ahead + behind) + (up + down)), NZ - 20)
            uz[k] = d - t if k == 0 else d + t
        if s > 0:
            faces = lax.fori_loop(0, NX, functools.partial(collide_plane, s), (blank, blank))
            zs[n + 2, 0], zs[n + 2, 1] = faces
            send("a", abuf.at[s - 1], n + 2)
        else:
            lax.fori_loop(0, NX, functools.partial(collide_plane, s), 0)

    last_copy = pltpu.make_async_copy(gbuf, grad, in_sem.at[0])
    last_copy.start()
    sent("f", fbuf, 0)
    for s in reversed(range(STEPS)):
        n = 1 + 2 * (STEPS - 1 - s)
        sent("a", abuf.at[s], n)
        sent("v", vbuf.at[s], n + 1)
    for x in range(NX):
        pltpu.make_async_copy(obuf.at[x], out.at[:, x], out_sem.at[x]).wait()
    last_copy.wait()


def solution(mesh):
    sizes = tuple(mesh.shape[a] for a in ("gx", "gy", "gz"))
    f32 = jnp.float32

    def per_device(cotangent, densities, velocities, adhesion, fluid):
        block = (NX, NY, NZ)
        return pl.pallas_call(
            functools.partial(kernel, sizes),
            out_shape=(jax.ShapeDtypeStruct((19,) + block, f32), jax.ShapeDtypeStruct(block, f32)),
            in_specs=[pl.BlockSpec(memory_space=pl.ANY)] * 5,
            out_specs=(pl.BlockSpec(memory_space=pl.ANY),) * 2,
            scratch_shapes=[
                pltpu.VMEM((19,) + block, f32),
                pltpu.VMEM((STEPS,) + block, f32),
                pltpu.VMEM((STEPS, 3) + block, f32),
                pltpu.VMEM(block, f32),
                pltpu.VMEM(block, jnp.int32),
                pltpu.VMEM((NX + 2, 4, 32, NZ), f32),
                pltpu.VMEM((STEPS, NX + 2, 20, 32, NZ), f32),
                pltpu.VMEM((STEPS, NX + 2, 3, 32, NZ), f32),
                pltpu.VMEM((NX, 19, NY, NZ), f32),
                pltpu.VMEM((NX, 4, NY, NZ), f32),
                pltpu.VMEM((NX, 18, NY, NZ), f32),
                pltpu.VMEM((NX, 19, NY, NZ), f32),
                pltpu.VMEM(block, f32),
                pltpu.VMEM((7, 2, NY, NZ), f32),
                pltpu.VMEM((7, 2, 32, NZ), f32),
                pltpu.VMEM((7, 2, 2, NY, NZ), f32),
                pltpu.VMEM((2, 3, NY, NZ), f32),
                pltpu.VMEM((2, NY, NZ), f32),
                pltpu.SemaphoreType.DMA((7, 18)),
                pltpu.SemaphoreType.DMA((7, 18)),
                pltpu.SemaphoreType.DMA((5,)),
                pltpu.SemaphoreType.DMA((NX,)),
            ],
            compiler_params=pltpu.CompilerParams(
                collective_id=0, has_side_effects=True, vmem_limit_bytes=48 * 1024 * 1024),
        )(cotangent, densities, velocities, adhesion, fluid)

    cells = P("gx", "gy", "gz")
    return jax.shard_map(
        per_device,
        mesh=mesh,
        in_specs=(P(None, "gx", "gy", "gz"), P(None, "gx", "gy", "gz"), P(None, None, "gx", "gy", "gz"), cells, cells),
        out_specs=(P(None, "gx", "gy", "gz"), cells),
        check_vma=False,
    )
```

profile of v0, /device:TPU:1, one launch (start us, length us, event | category | flops | bytes accessed | tf_op | source)
XLA Modules:
  0.0 46.6 jit_solution(13449714281897566336)
XLA Ops:
  0.6 0.0 copy-start
  0.6 1.3 %copy-done = f32[19,8,16,128]{3,2,1,0:T(8,128)S(1)} copy-done((f32[19,8,16,128]{3,2,1,0:T(8,128)S(1)}, f32[19,8,16,128]{3,2,1,0:T(8,128)}, u32[]{:S(2)}) %copy-start) | copy-done | bytes 1245208
  1.9 0.0 copy-start.1
  1.9 1.1 %copy-done.1 = f32[3,3,8,16,128]{4,3,2,1,0:T(8,128)S(1)} copy-done((f32[3,3,8,16,128]{4,3,2,1,0:T(8,128)S(1)}, f32[3,3,8,16,128]{4,3,2,1,0:T(8,128)}, u32[]{:S(2)}) %copy-start.1) | copy-done | bytes 589848
  3.0 0.0 copy-start.2
  3.0 0.9 %copy-done.2 = f32[3,8,16,128]{3,2,1,0:T(8,128)S(1)} copy-done((f32[3,8,16,128]{3,2,1,0:T(8,128)S(1)}, f32[3,8,16,128]{3,2,1,0:T(8,128)}, u32[]{:S(2)}) %copy-start.2) | copy-done | bytes 196632
  3.9 0.0 copy-start.3
  3.9 0.8 %copy-done.3 = f32[8,16,128]{2,1,0:T(8,128)S(1)} copy-done((f32[8,16,128]{2,1,0:T(8,128)S(1)}, f32[8,16,128]{2,1,0:T(8,128)}, u32[]{:S(2)}) %copy-start.3) | copy-done | bytes 65560
  4.8 0.0 copy-start.4
  4.8 0.8 %copy-done.4 = s32[8,16,128]{2,1,0:T(8,128)S(1)} copy-done((s32[8,16,128]{2,1,0:T(8,128)S(1)}, s32[8,16,128]{2,1,0:T(8,128)}, u32[]{:S(2)}) %copy-start.4) | copy-done | bytes 65560
  5.6 39.3 %shard_map.68 = (f32[19,8,16,128]{3,2,1,0:T(8,128)S(1)}, f32[8,16,128]{2,1,0:T(8,128)S(1)}) custom-call(f32[19,8,16,128]{3,2,1,0:T(8,128)S(1)} %copy-done, f32[3,8,16,128]{3,2,1,0:T(8,128)S(1)} %copy-done.2, f32[3,3,8,16,128]{4,3,2,1,0:T(8,128)S(1)} %copy-done.1, f32[8,16,128]{2,1,0:T(8,128)S(1)} %copy-done.3, s32[8,16,128]{2,1,0:T(8,128)S(1)} %copy-done.4), custom_call_target="tpu_custom_call" | custom-call | tf_op jit(solution)/shard_map/pallas_call | solution.py:406
  44.9 1.0 %copy.9 = f32[19,8,16,128]{3,2,1,0:T(8,128)} copy(f32[19,8,16,128]{3,2,1,0:T(8,128)S(1)} %get-tuple-element.4) | data formatting | bytes 2490368
  45.9 0.6 %copy.10 = f32[8,16,128]{2,1,0:T(8,128)} copy(f32[8,16,128]{2,1,0:T(8,128)S(1)} %get-tuple-element.5) | data formatting | bytes 131072
Async XLA Ops:
  0.6 1.3 %copy-start = (f32[19,8,16,128]{3,2,1,0:T(8,128)S(1)}, f32[19,8,16,128]{3,2,1,0:T(8,128)}, u32[]{:S(2)}) copy-start(f32[19,8,16,128]{3,2,1,0:T(8,128)} %cot.1) | copy-start | bytes 3735556
  1.9 1.1 %copy-start.1 = (f32[3,3,8,16,128]{4,3,2,1,0:T(8,128)S(1)}, f32[3,3,8,16,128]{4,3,2,1,0:T(8,128)}, u32[]{:S(2)}) copy-start(f32[3,3,8,16,128]{4,3,2,1,0:T(8,128)} %vel.1) | copy-start | bytes 1769476
  3.0 0.9 %copy-start.2 = (f32[3,8,16,128]{3,2,1,0:T(8,128)S(1)}, f32[3,8,16,128]{3,2,1,0:T(8,128)}, u32[]{:S(2)}) copy-start(f32[3,8,16,128]{3,2,1,0:T(8,128)} %dens.1) | copy-start | bytes 589828
  3.9 0.8 %copy-start.3 = (f32[8,16,128]{2,1,0:T(8,128)S(1)}, f32[8,16,128]{2,1,0:T(8,128)}, u32[]{:S(2)}) copy-start(f32[8,16,128]{2,1,0:T(8,128)} %adh.1) | copy-start | bytes 196612
  4.8 0.8 %copy-start.4 = (s32[8,16,128]{2,1,0:T(8,128)S(1)}, s32[8,16,128]{2,1,0:T(8,128)}, u32[]{:S(2)}) copy-start(s32[8,16,128]{2,1,0:T(8,128)} %flu.1) | copy-start | bytes 196612
where the time goes:
time: 46.9 us; the launch traced here: 46.6 us
  Pallas kernels  39.3 us (84%)
  local copies, waits for them, and re-layouts  6.62 us (14%)
  between operations  0.65 us (1%)
    pallas_call x1, Pallas kernels, per_device(): pl.pallas_call(functools.partial(kernel, sizes), out_shape=(jax.ShapeDtyp...  39.3 us
    unnamed x12, local copies, waits for them, and re-layouts  6.62 us

commit v1 on v0

--- a/solution.py
+++ b/solution.py
@@ -57,7 +57,7 @@
 
 def kernel(sizes, cot, dens, vel, adh, flu, out, grad,
            cbuf, dbuf, ubuf, adbuf, fibuf, fbuf, abuf, vbuf, bbuf, mbuf, nbuf, obuf, gbuf,
-           zs, zr, ze, hz, uz, send_sem, recv_sem, in_sem, out_sem):
+           zs, zr, ze, hz, uz, wbuf, send_sem, recv_sem, in_sem, out_sem):
     index = [lax.axis_index(a) for a in ("gx", "gy", "gz")]
     lane = lax.broadcasted_iota(jnp.int32, (NY, NZ), 1)
     first, last = lane == 0, lane == NZ - 1
@@ -76,6 +76,7 @@
         return tuple(index[axis] + d[axis] for axis in range(3))
 
     here = {d: present(d) for d in NEIGHBOURS}
+    along = [sum(here[d].astype(jnp.int32) for d in NEIGHBOURS if sum(map(abs, d)) == 1 and d[axis]) for axis in range(3)]
 
     def message(kind, buf, n, d):
         dx, dy, dz = d
@@ -100,25 +101,30 @@
         ys = (pl.ds(0, 1), pl.ds(24, 1)) if dy < 0 else (pl.ds(15, 1), pl.ds(7, 1))
         return zs.at[n, k, ys[0]], zr.at[n, k, ys[1]]
 
-    def copy(kind, buf, n, d, to):
+    def copy(kind, buf, n, d):
         source, target = message(kind, buf, n, d)
-        j = NEIGHBOURS.index(d)
         return pltpu.make_async_remote_copy(
-            src_ref=source, dst_ref=target, send_sem=send_sem.at[n, j], recv_sem=recv_sem.at[n, j],
-            device_id=device(to), device_id_type=MESH)
+            src_ref=source, dst_ref=target, send_sem=send_sem.at[n], recv_sem=recv_sem.at[n],
+            device_id=device(d), device_id_type=MESH)
 
     def send(kind, buf, n):
         for d in NEIGHBOURS:
             @pl.when(here[d])
             def _():
-                copy(kind, buf, n, d, d).start()
+                copy(kind, buf, n, d).start()
+
+    def await_rows(kind, sem):
+        fields = {"f": 4, "a": 5, "v": 3}[kind]
+        edge = 1 if kind == "a" else fields
+        for counts in itertools.product((1, 2), repeat=3):
+            rows = sum(t * size for t, size in zip(counts, (fields * NY, fields * NX, NY)))
+            rows += counts[0] * counts[1] * edge + counts[0] * counts[2] * NY + counts[1] * counts[2]
+            @pl.when(functools.reduce(jnp.logical_and, [t == c for t, c in zip(along, counts)]))
+            def _():
+                pltpu.make_async_copy(wbuf.at[0, pl.ds(0, rows)], wbuf.at[1, pl.ds(0, rows)], sem).wait()
 
     def receive(kind, buf, n, fields):
-        for d in NEIGHBOURS:
-            source = tuple(-t for t in d)
-            @pl.when(here[source])
-            def _():
-                copy(kind, buf, n, d, source).wait_recv()
+        await_rows(kind, recv_sem.at[n])
         right = functools.reduce(jnp.logical_or, [lane == position(f, NX) for f in range(fields)])
         left = functools.reduce(jnp.logical_or, [lane == position(f, -1) for f in range(fields)])
         for k in range(2):
@@ -127,11 +133,8 @@
             face = jnp.where(left, rolled(ze[n, k, 1], NZ - 8), face)
             zr[n, k, OWN, :] = face
 
-    def sent(kind, buf, n):
-        for d in NEIGHBOURS:
-            @pl.when(here[d])
-            def _():
-                copy(kind, buf, n, d, d).wait_send()
+    def sent(kind, n):
+        await_rows(kind, send_sem.at[n])
 
     def pack(faces, field, x, low, high):
         at = position(field, x)
@@ -257,6 +260,7 @@
         return carry
 
     lax.fori_loop(0, NX, flags, 0)
+    sent("f", 0)
     loads[4].wait()
 
     def stream_plane(s, n, x, faces):
@@ -370,6 +374,8 @@
         zs[n + 1, 0], zs[n + 1, 1] = faces
         send("v", v, n + 1)
         lax.fori_loop(0, NX, functools.partial(force_plane, s), 0)
+        sent("a", n)
+        sent("v", n + 1)
         receive("v", v, n + 1, 3)
         for k in range(2):
             face = zr[n + 1, k, OWN, :]
@@ -387,11 +393,6 @@
 
     last_copy = pltpu.make_async_copy(gbuf, grad, in_sem.at[0])
     last_copy.start()
-    sent("f", fbuf, 0)
-    for s in reversed(range(STEPS)):
-        n = 1 + 2 * (STEPS - 1 - s)
-        sent("a", abuf.at[s], n)
-        sent("v", vbuf.at[s], n + 1)
     for x in range(NX):
         pltpu.make_async_copy(obuf.at[x], out.at[:, x], out_sem.at[x]).wait()
     last_copy.wait()
@@ -406,8 +407,8 @@
         return pl.pallas_call(
             functools.partial(kernel, sizes),
             out_shape=(jax.ShapeDtypeStruct((19,) + block, f32), jax.ShapeDtypeStruct(block, f32)),
-            in_specs=[pl.BlockSpec(memory_space=pl.ANY)] * 5,
-            out_specs=(pl.BlockSpec(memory_space=pl.ANY),) * 2,
+            in_specs=[pl.BlockSpec(memory_space=pltpu.HBM)] * 5,
+            out_specs=(pl.BlockSpec(memory_space=pltpu.HBM),) * 2,
             scratch_shapes=[
                 pltpu.VMEM((19,) + block, f32),
                 pltpu.VMEM((STEPS,) + block, f32),
@@ -427,14 +428,15 @@
                 pltpu.VMEM((7, 2, 2, NY, NZ), f32),
                 pltpu.VMEM((2, 3, NY, NZ), f32),
                 pltpu.VMEM((2, NY, NZ), f32),
-                pltpu.SemaphoreType.DMA((7, 18)),
-                pltpu.SemaphoreType.DMA((7, 18)),
+                pltpu.VMEM((2, 400, NZ), f32),
+                pltpu.SemaphoreType.DMA((7,)),
+                pltpu.SemaphoreType.DMA((7,)),
                 pltpu.SemaphoreType.DMA((5,)),
                 pltpu.SemaphoreType.DMA((NX,)),
             ],
             compiler_params=pltpu.CompilerParams(
                 collective_id=0, has_side_effects=True, vmem_limit_bytes=48 * 1024 * 1024),
-        )(cotangent, densities, velocities, adhesion, fluid)
+        )(*[pltpu.with_memory_space_constraint(t, pltpu.HBM) for t in (cotangent, densities, velocities, adhesion, fluid)])
 
     cells = P("gx", "gy", "gz")
     return jax.shard_map(

time: 46.9 us -> 39.4 us (0.84)
  local copies, waits for them, and re-layouts: 6.62 us -> 1.67 us
  Pallas kernels: 39.3 us -> 37 us
    unnamed x12 -> x2, local copies, waits for them, and re-layouts: 6.62 us -> 1.67 us
    pallas_call x1, Pallas kernels: 39.3 us -> 37 us  [per_device(): pl.pallas_call(functools.partial(kernel, sizes), out_shape=(jax.ShapeDtyp...]
where the time goes in v1:
time: 39.4 us; the launch traced here: 39.3 us
  Pallas kernels  37 us (94%)
  local copies, waits for them, and re-layouts  1.67 us (4%)
  between operations  0.64 us (2%)
    pallas_call x1, Pallas kernels, per_device(): pl.pallas_call(functools.partial(kernel, sizes), out_shape=(jax.ShapeDtyp...  37 us
    unnamed x2, local copies, waits for them, and re-layouts  1.67 us

profile of v1, /device:TPU:1, one launch (start us, length us, event | category | flops | bytes accessed | tf_op | source)
XLA Modules:
  0.0 39.3 jit_solution(8484176171742759084)
XLA Ops:
  0.6 37.0 %shard_map.68 = (f32[19,8,16,128]{3,2,1,0:T(8,128)S(1)}, f32[8,16,128]{2,1,0:T(8,128)S(1)}) custom-call(f32[19,8,16,128]{3,2,1,0:T(8,128)} %cot.1, f32[3,8,16,128]{3,2,1,0:T(8,128)} %dens.1, f32[3,3,8,16,128]{4,3,2,1,0:T(8,128)} %vel.1, f32[8,16,128]{2,1,0:T(8,128)} %adh.1, s32[8,16,128]{2,1,0:T(8,128)} %flu.1), custom_call_target="tpu_custom_call" | custom-call | tf_op jit(solution)/shard_map/pallas_call | solution.py:407
  37.6 1.0 %copy.9 = f32[19,8,16,128]{3,2,1,0:T(8,128)} copy(f32[19,8,16,128]{3,2,1,0:T(8,128)S(1)} %get-tuple-element.4) | data formatting | bytes 2490368
  38.6 0.6 %copy.10 = f32[8,16,128]{2,1,0:T(8,128)} copy(f32[8,16,128]{2,1,0:T(8,128)S(1)} %get-tuple-element.5) | data formatting | bytes 131072

commit v2 on v1

--- a/solution.py
+++ b/solution.py
@@ -57,7 +57,7 @@
 
 def kernel(sizes, cot, dens, vel, adh, flu, out, grad,
            cbuf, dbuf, ubuf, adbuf, fibuf, fbuf, abuf, vbuf, bbuf, mbuf, nbuf, obuf, gbuf,
-           zs, zr, ze, hz, uz, wbuf, send_sem, recv_sem, in_sem, out_sem):
+           zs, zx, zr, ze, hz, uz, wbuf, send_sem, recv_sem, in_sem, out_sem):
     index = [lax.axis_index(a) for a in ("gx", "gy", "gz")]
     lane = lax.broadcasted_iota(jnp.int32, (NY, NZ), 1)
     first, last = lane == 0, lane == NZ - 1
@@ -95,7 +95,7 @@
             return buf.at[xs[0], slots, ys[0]], buf.at[xs[1], slots, ys[1]]
         k = 0 if dz < 0 else 1
         if dx != 0:
-            return zs.at[n, k], ze.at[n, k, 0 if dx < 0 else 1]
+            return zx.at[n, k], ze.at[n, k, 0 if dx < 0 else 1]
         if dy == 0:
             return zs.at[n, k], zr.at[n, k, OWN]
         ys = (pl.ds(0, 1), pl.ds(24, 1)) if dy < 0 else (pl.ds(15, 1), pl.ds(7, 1))
@@ -107,8 +107,10 @@
             src_ref=source, dst_ref=target, send_sem=send_sem.at[n], recv_sem=recv_sem.at[n],
             device_id=device(d), device_id_type=MESH)
 
-    def send(kind, buf, n):
+    def send(kind, buf, n, along_x):
         for d in NEIGHBOURS:
+            if (d[0] != 0) != along_x:
+                continue
             @pl.when(here[d])
             def _():
                 copy(kind, buf, n, d).start()
@@ -136,6 +138,16 @@
     def sent(kind, n):
         await_rows(kind, send_sem.at[n])
 
+    def planes(plane, kind, buf, n, wait=None):
+        faces = lax.fori_loop(0, 2, lambda i, carry: plane((NX - 1) * i, carry), (blank, blank), unroll=2)
+        zx[n, 0], zx[n, 1] = faces
+        if wait is not None:
+            wait()
+        send(kind, buf, n, True)
+        faces = lax.fori_loop(1, NX - 1, plane, faces, unroll=NX - 2)
+        zs[n, 0], zs[n, 1] = faces
+        send(kind, buf, n, False)
+
     def pack(faces, field, x, low, high):
         at = position(field, x)
         mine = lane == at
@@ -152,17 +164,17 @@
             return jnp.where(last, rolled(packed, NZ - 1 - at), rolled(values, NZ - 1))
         return jnp.where(first, rolled(packed, NZ - at), rolled(values, 1))
 
-    barrier = pltpu.get_barrier_semaphore()
-    for d in NEIGHBOURS:
-        @pl.when(here[d])
-        def _():
-            pl.semaphore_signal(barrier, inc=1, device_id=device(d), device_id_type=MESH)
     loads = [
         pltpu.make_async_copy(source, target, in_sem.at[k])
         for k, (source, target) in enumerate(((flu, fibuf), (adh, adbuf), (dens, dbuf), (cot, cbuf), (vel, ubuf)))
     ]
     for load in loads:
         load.start()
+    barrier = pltpu.get_barrier_semaphore()
+    for d in NEIGHBOURS:
+        @pl.when(here[d])
+        def _():
+            pl.semaphore_signal(barrier, inc=1, device_id=device(d), device_id_type=MESH)
     blank = jnp.zeros((NY, NZ), jnp.float32)
     row = jnp.zeros((1, NZ), jnp.float32)
     for e, d in enumerate(((1, 0, 0), (-1, 0, 0))):
@@ -214,10 +226,10 @@
             faces = pack(faces, f, x, value, value)
         return faces
 
-    faces = lax.fori_loop(0, NX, fixed, (blank, blank))
-    zs[0, 0], zs[0, 1] = faces
-    pl.semaphore_wait(barrier, sum(here[d].astype(jnp.int32) for d in NEIGHBOURS))
-    send("f", fbuf, 0)
+    def greeted():
+        pl.semaphore_wait(barrier, sum(here[d].astype(jnp.int32) for d in NEIGHBOURS))
+
+    planes(fixed, "f", fbuf, 0, greeted)
 
     loads[3].wait()
 
@@ -236,9 +248,7 @@
         fl = fbuf[x + 1, 0, OWN, :]
         return store_plane(abuf.at[STEPS - 1], x, {c: fl * cbuf[i, x] for i, c in enumerate(DIRECTIONS)}, faces)
 
-    faces = lax.fori_loop(0, NX, masked, (blank, blank))
-    zs[1, 0], zs[1, 1] = faces
-    send("a", abuf.at[STEPS - 1], 1)
+    planes(masked, "a", abuf.at[STEPS - 1], 1)
 
     receive("f", fbuf, 0, 4)
     for k in range(2):
@@ -370,9 +380,7 @@
         receive("a", a, n, 5)
         for x in range(NX):
             a[x + 1, SLOT[(1, -1, 0)], 7:8, :] = a[x + 1, COPY, 7:8, :]
-        faces = lax.fori_loop(0, NX, functools.partial(stream_plane, s, n), (blank, blank))
-        zs[n + 1, 0], zs[n + 1, 1] = faces
-        send("v", v, n + 1)
+        planes(functools.partial(stream_plane, s, n), "v", v, n + 1)
         lax.fori_loop(0, NX, functools.partial(force_plane, s), 0)
         sent("a", n)
         sent("v", n + 1)
@@ -385,11 +393,9 @@
             t = rolled(W1 * face + W2 * ((ahead + behind) + (up + down)), NZ - 20)
             uz[k] = d - t if k == 0 else d + t
         if s > 0:
-            faces = lax.fori_loop(0, NX, functools.partial(collide_plane, s), (blank, blank))
-            zs[n + 2, 0], zs[n + 2, 1] = faces
-            send("a", abuf.at[s - 1], n + 2)
+            planes(functools.partial(collide_plane, s), "a", abuf.at[s - 1], n + 2)
         else:
-            lax.fori_loop(0, NX, functools.partial(collide_plane, s), 0)
+            lax.fori_loop(0, NX, functools.partial(collide_plane, s), 0, unroll=8)
 
     last_copy = pltpu.make_async_copy(gbuf, grad, in_sem.at[0])
     last_copy.start()
@@ -424,6 +430,7 @@
                 pltpu.VMEM((NX, 19, NY, NZ), f32),
                 pltpu.VMEM(block, f32),
                 pltpu.VMEM((7, 2, NY, NZ), f32),
+                pltpu.VMEM((7, 2, NY, NZ), f32),
                 pltpu.VMEM((7, 2, 32, NZ), f32),
                 pltpu.VMEM((7, 2, 2, NY, NZ), f32),
                 pltpu.VMEM((2, 3, NY, NZ), f32),

time: 39.4 us -> 34.4 us (0.87)
  Pallas kernels: 37 us -> 31.9 us
    pallas_call x1, Pallas kernels: 37 us -> 31.9 us  [per_device(): pl.pallas_call(functools.partial(kernel, sizes), out_shape=(jax.ShapeDtyp...]
where the time goes in v2:
time: 34.4 us; the launch traced here: 34.2 us
  Pallas kernels  31.9 us (93%)
  local copies, waits for them, and re-layouts  1.67 us (5%)
  between operations  0.64 us (2%)
    pallas_call x1, Pallas kernels, per_device(): pl.pallas_call(functools.partial(kernel, sizes), out_shape=(jax.ShapeDtyp...  31.9 us
    unnamed x2, local copies, waits for them, and re-layouts  1.67 us

profile of v2, /device:TPU:1, one launch (start us, length us, event | category | flops | bytes accessed | tf_op | source)
XLA Modules:
  0.0 34.2 jit_solution(18312278931751362390)
XLA Ops:
  0.6 31.9 %shard_map.68 = (f32[19,8,16,128]{3,2,1,0:T(8,128)S(1)}, f32[8,16,128]{2,1,0:T(8,128)S(1)}) custom-call(f32[19,8,16,128]{3,2,1,0:T(8,128)} %cot.1, f32[3,8,16,128]{3,2,1,0:T(8,128)} %dens.1, f32[3,3,8,16,128]{4,3,2,1,0:T(8,128)} %vel.1, f32[8,16,128]{2,1,0:T(8,128)} %adh.1, s32[8,16,128]{2,1,0:T(8,128)} %flu.1), custom_call_target="tpu_custom_call" | custom-call | tf_op jit(solution)/shard_map/pallas_call | solution.py:413
  32.6 1.0 %copy.9 = f32[19,8,16,128]{3,2,1,0:T(8,128)} copy(f32[19,8,16,128]{3,2,1,0:T(8,128)S(1)} %get-tuple-element.4) | data formatting | bytes 2490368
  33.6 0.6 %copy.10 = f32[8,16,128]{2,1,0:T(8,128)} copy(f32[8,16,128]{2,1,0:T(8,128)S(1)} %get-tuple-element.5) | data formatting | bytes 131072

commit v3 on v2

v3 whole, which is shorter than its diff:
```python
import functools
import itertools

import jax
import jax.numpy as jnp
from jax import lax
from jax.experimental import pallas as pl
from jax.experimental.pallas import tpu as pltpu
from jax.sharding import PartitionSpec as P

DIRECTIONS = (
    (0, 0, 0), (1, 0, 0), (-1, 0, 0), (0, 1, 0), (0, -1, 0), (0, 0, 1), (0, 0, -1),
    (1, 1, 0), (-1, -1, 0), (1, -1, 0), (-1, 1, 0),
    (1, 0, 1), (-1, 0, -1), (1, 0, -1), (-1, 0, 1),
    (0, 1, 1), (0, -1, -1), (0, 1, -1), (0, -1, 1),
)
W0, W1, W2 = 1.0 / 3.0, 1.0 / 18.0, 1.0 / 36.0
TAU = 0.8
G = -5.0
STEPS = 3
NX, NY, NZ = 8, 16, 128
MESH = pl.DeviceIdType.MESH

SLOTS = (
    (1, -1, 0), (1, 0, 0), (1, 0, 1), (1, 0, -1), (1, 1, 0),
    (0, 1, 0), (0, 1, 1), (0, 1, -1),
    (-1, 1, 0), (-1, 0, 0), (-1, 0, -1), (-1, 0, 1), (-1, -1, 0),
    (0, -1, 0), (0, -1, -1), (0, -1, 1),
    None,
    (0, 0, 1), (0, 0, -1), (0, 0, 0),
)
SLOT = {c: k for k, c in enumerate(SLOTS) if c is not None}
COPY = 16
ZPOP = (
    ((0, 0, 1), (1, 0, 1), (-1, 0, 1), (0, 1, 1), (0, -1, 1)),
    ((0, 0, -1), (1, 0, -1), (-1, 0, -1), (0, 1, -1), (0, -1, -1)),
)
PAIRS = tuple((c, tuple(-t for t in c)) for c in DIRECTIONS[1::2])
NEIGHBOURS = sorted(
    (d for d in itertools.product((-1, 0, 1), repeat=3) if any(d)),
    key=lambda d: (-abs(d[0]), d[2] != 0, sum(map(abs, d))))
BLOCKS = ((8, NY), (7, 1), (24, 1))
KINDS = ("f", "a", "m", "m", "v")
ROWS = {
    "f": {(1, 0, 0): 64, (0, 1, 0): 32, (0, 0, 1): 16, (1, 1, 0): 4, (1, 0, 1): 16, (0, 1, 1): 1},
    "a": {(1, 0, 0): 80, (0, 1, 0): 40, (0, 0, 1): 16, (1, 1, 0): 1, (1, 0, 1): 16, (0, 1, 1): 1},
    "m": {(1, 0, 0): 176, (0, 1, 0): 88, (0, 0, 1): 32, (1, 1, 0): 13, (1, 0, 1): 32, (0, 1, 1): 4, (1, 1, 1): 2},
    "v": {(1, 0, 0): 48, (0, 1, 0): 24, (0, 0, 1): 16, (1, 1, 0): 3, (1, 0, 1): 16, (0, 1, 1): 1},
}
OWN = pl.ds(8, NY)


def position(field, x):
    return 4 + 20 * field + 2 * x


def v_position(k, x):
    return 4 + 24 * k + 2 * x


def rolled(values, shift):
    return pltpu.roll(values, shift, 1)


def back_by(values, lanes):
    return values if lanes == 0 else pltpu.roll(values, NZ - lanes, 1)


def kernel(sizes, cot, dens, vel, adh, flu, out, grad,
           cbuf, dbuf, ubuf, adbuf, fibuf, fbuf, abuf, vbuf, pbuf, nbuf, obuf, gbuf, cor,
           zs, zx, zr, ze, hz, uz, zb, wbuf, send_sem, recv_sem, in_sem, out_sem):
    index = [lax.axis_index(a) for a in ("gx", "gy", "gz")]
    lane = lax.broadcasted_iota(jnp.int32, (NY, NZ), 1)
    lane_row = lax.broadcasted_iota(jnp.int32, (1, NZ), 1)

    def lanes_of(values):
        return lane if values.shape[0] == NY else lane_row

    def present(d):
        found = None
        for axis in range(3):
            if d[axis] == 0:
                continue
            at = index[axis] + d[axis]
            inside = at >= 0 if d[axis] < 0 else at < sizes[axis]
            found = inside if found is None else jnp.logical_and(found, inside)
        return found

    def device(d):
        return tuple(index[axis] + d[axis] for axis in range(3))

    here = {d: present(d) for d in NEIGHBOURS}
    along = [sum(here[d].astype(jnp.int32) for d in NEIGHBOURS if sum(map(abs, d)) == 1 and d[axis]) for axis in range(3)]

    def messages(n, d, a, v):
        kind = KINDS[n]
        dx, dy, dz = d
        axes = tuple(map(abs, d))
        if axes not in ROWS[kind]:
            return []
        deep = 2 if kind == "m" else 1
        if dz == 0:
            pairs = []
            if kind != "v":
                if kind == "f":
                    slots = pl.ds(0, 4)
                elif dx == 0:
                    slots = pl.ds(4, 5) if dy < 0 else pl.ds(12, 5)
                elif dy == 0:
                    slots = pl.ds(0, 5) if dx < 0 else pl.ds(8, 5)
                else:
                    slots = pl.ds(SLOT[(-dx, -dy, 0)], 1)
                xs = (pl.ds(1, NX),) * 2 if dx == 0 else ((pl.ds(1, 1), pl.ds(9, 1)) if dx < 0 else (pl.ds(8, 1), pl.ds(0, 1)))
                ys = (OWN,) * 2 if dy == 0 else ((pl.ds(8, 1), pl.ds(24, 1)) if dy < 0 else (pl.ds(23, 1), pl.ds(7, 1)))
                buf = fbuf if kind == "f" else a
                pairs.append((buf.at[xs[0], slots, ys[0]], buf.at[xs[1], slots, ys[1]]))
            if kind in "mv":
                if dx == 0:
                    xs = (pl.ds(2, NX),) * 2
                else:
                    xs = (pl.ds(2, deep), pl.ds(10, deep)) if dx < 0 else (pl.ds(10 - deep, deep), pl.ds(2 - deep, deep))
                if dy == 0:
                    ys = (OWN,) * 2
                else:
                    ys = (pl.ds(8, deep), pl.ds(24, deep)) if dy < 0 else (pl.ds(24 - deep, deep), pl.ds(8 - deep, deep))
                pairs.append((v.at[xs[0], pl.ds(0, 3), ys[0]], v.at[xs[1], pl.ds(0, 3), ys[1]]))
            return pairs
        k = 0 if dz < 0 else 1
        e = 0 if dx < 0 else 1
        parts = {"f": pl.ds(0, 1), "a": pl.ds(0, 1), "m": pl.ds(0, 2), "v": pl.ds(1, 1)}[kind]
        if dy != 0:
            ys = (pl.ds(0, deep), pl.ds(24, deep)) if dy < 0 else (pl.ds(NY - deep, deep), pl.ds(8 - deep, deep))
        else:
            ys = (pl.ds(0, NY), OWN)
        if dx == 0:
            return [(zs.at[n, k, parts, ys[0]], zr.at[n, k, parts, ys[1]])]
        if dy != 0:
            parts = pl.ds(1, 1)
        return [(zx.at[n, k, parts, ys[0]], ze.at[n, k, e, parts, ys[1]])]

    def send(n, a, v, along_x):
        for d in NEIGHBOURS:
            pairs = messages(n, d, a, v)
            if (d[0] != 0) != along_x or not pairs:
                continue
            @pl.when(here[d])
            def _():
                for source, target in pairs:
                    pltpu.make_async_remote_copy(
                        src_ref=source, dst_ref=target, send_sem=send_sem.at[n], recv_sem=recv_sem.at[n],
                        device_id=device(d), device_id_type=MESH).start()

    def await_rows(n, sem):
        for counts in itertools.product((1, 2), repeat=3):
            rows = 0
            for axes, size in ROWS[KINDS[n]].items():
                for t, used in zip(counts, axes):
                    size = size * t if used else size
                rows += size
            @pl.when(functools.reduce(jnp.logical_and, [t == c for t, c in zip(along, counts)]))
            def _():
                pltpu.make_async_copy(wbuf.at[0, pl.ds(0, rows)], wbuf.at[1, pl.ds(0, rows)], sem.at[n]).wait()

    def receive(n):
        await_rows(n, recv_sem)
        kind = KINDS[n]
        ranges = []
        if kind != "v":
            fields = 4 if kind == "f" else 5
            ranges.append((0, [position(f, NX) for f in range(fields)], [position(f, -1) for f in range(fields)], 1))
        if kind in "mv":
            ranges.append((1, [v_position(f, NX) for f in range(3)], [v_position(f, -2) for f in range(3)], 4))
        for part, rights, lefts, width in ranges:
            inside = lambda at: jnp.logical_and(lane >= at, lane < at + width)
            right = functools.reduce(jnp.logical_or, [inside(at) for at in rights])
            left = functools.reduce(jnp.logical_or, [inside(at) for at in lefts])
            rows = (0, 16) if part == 1 else (8,)
            for k in range(2):
                for r in rows:
                    face = zr[n, k, part, r:r + 16, :]
                    face = jnp.where(right, rolled(ze[n, k, 0, part, r:r + 16, :], 16), face)
                    face = jnp.where(left, rolled(ze[n, k, 1, part, r:r + 16, :], NZ - 16), face)
                    zr[n, k, part, r:r + 16, :] = face

    def sent(n):
        await_rows(n, send_sem)

    def planes(plane, n, a=None, v=None, wait=None):
        faces = tuple((blank,) * 2 for part in range(2))
        for x in (0, NX - 2):
            faces = lax.fori_loop(x, x + 2, plane, faces, unroll=2)
        for part in range(2):
            for k in range(2):
                zx[n, k, part] = faces[part][k]
        if wait is not None:
            wait()
        send(n, a, v, True)
        faces = lax.fori_loop(2, NX - 2, plane, faces, unroll=NX - 4)
        for part in range(2):
            for k in range(2):
                zs[n, k, part] = faces[part][k]
        send(n, a, v, False)

    def pack(faces, at, low, high):
        mine = lane == at
        zero, one = faces
        if low is not None:
            zero = jnp.where(mine, rolled(low, at), zero)
        if high is not None:
            one = jnp.where(mine, rolled(high, at + 1), one)
        return zero, one

    def pack_v(faces, at, value):
        mine = jnp.logical_or(lane == at, lane == at + 1)
        return jnp.where(mine, rolled(value, at), faces[0]), jnp.where(mine, rolled(value, at + 2), faces[1])

    def moved(values, packed, at, cz):
        if cz > 0:
            return jnp.where(lanes_of(values) == NZ - 1, rolled(packed, NZ - 1 - at), rolled(values, NZ - 1))
        return jnp.where(lanes_of(values) == 0, rolled(packed, NZ - at), rolled(values, 1))

    loads = [
        pltpu.make_async_copy(source, target, in_sem.at[k])
        for k, (source, target) in enumerate(((flu, fibuf), (adh, adbuf), (dens, dbuf), (cot, cbuf), (vel, ubuf)))
    ]
    for load in loads:
        load.start()
    barrier = pltpu.get_barrier_semaphore()
    for d in NEIGHBOURS:
        @pl.when(here[d])
        def _():
            pl.semaphore_signal(barrier, inc=1, device_id=device(d), device_id_type=MESH)
    blank = jnp.zeros((NY, NZ), jnp.float32)
    row = jnp.zeros((1, NZ), jnp.float32)
    two_rows = jnp.zeros((2, NZ), jnp.float32)
    needed = ((0, 0), (2, 1), (3, 1), (4, 1))
    for e, d in enumerate(((1, 0, 0), (-1, 0, 0))):
        @pl.when(jnp.logical_not(here[d]))
        def _():
            for r in (0, 16):
                for f in range(4):
                    fbuf[NX + 1 if e == 0 else 0, f, r:r + 16, :] = blank
                for q in ((10, 11) if e == 0 else (0, 1)):
                    for f in range(3):
                        for s in range(STEPS):
                            vbuf[s, q, f, r:r + 16, :] = blank
                for n, part in needed:
                    for k in range(2):
                        ze[n, k, e, part, r:r + 16, :] = blank
    for r, d in ((24, (0, 1, 0)), (6, (0, -1, 0))):
        @pl.when(jnp.logical_not(here[d]))
        def _():
            for p in range(NX + 2):
                for f in range(4):
                    fbuf[p, f, r:r + 2, :] = two_rows
            for q in range(NX + 4):
                for f in range(3):
                    for s in range(STEPS):
                        vbuf[s, q, f, r:r + 2, :] = two_rows
            for n, part in needed:
                for k in range(2):
                    zr[n, k, part, r:r + 2, :] = two_rows
                    for e in range(2):
                        ze[n, k, e, part, r:r + 2, :] = two_rows
    for k, d in enumerate(((0, 0, 1), (0, 0, -1))):
        @pl.when(jnp.logical_not(here[d]))
        def _():
            for n, part in needed:
                for r in (0, 16):
                    zr[n, k, part, r:r + 16, :] = blank
                    for e in range(2):
                        ze[n, k, e, part, r:r + 16, :] = blank

    for k in range(3):
        loads[k].wait()

    def fixed(x, faces):
        fl = fibuf[x].astype(jnp.float32)
        wall = (1.0 - fl) * adbuf[x]
        fields = [fl]
        packed = faces[0]
        for s in range(STEPS):
            fields.append(fl * (G * (1.0 - jnp.exp(-dbuf[s, x]))) + wall)
        for f, value in enumerate(fields):
            fbuf[x + 1, f, OWN, :] = value
            packed = pack(packed, position(f, x), value, value)
        return packed, faces[1]

    def greeted():
        pl.semaphore_wait(barrier, sum(here[d].astype(jnp.int32) for d in NEIGHBOURS))

    planes(fixed, 0, wait=greeted)

    loads[3].wait()

    def store_plane(buf, x, populations, packed):
        for c, value in populations.items():
            buf[x + 1, SLOT[c], OWN, :] = value
            if c == (1, -1, 0):
                buf[x + 1, COPY, 16:24, :] = value[8:16]
        for k in range(2):
            for j, c in enumerate(ZPOP[k]):
                value = populations[c]
                packed = pack(packed, position(j, x), value if k == 0 else None, value if k == 1 else None)
        return packed

    def masked(x, faces):
        fl = fbuf[x + 1, 0, OWN, :]
        packed = store_plane(abuf.at[STEPS - 1], x, {c: fl * cbuf[i, x] for i, c in enumerate(DIRECTIONS)}, faces[0])
        return packed, faces[1]

    planes(masked, 1, a=abuf.at[STEPS - 1])

    receive(0)
    for k in range(2):
        face = zr[0, k, 0, OWN, :]
        up, down = zr[0, k, 0, 9:25, :], zr[0, k, 0, 7:23, :]
        ahead, behind = rolled(face, NZ - 2), rolled(face, 2)
        hz[k, 0] = ahead - behind
        hz[k, 1] = up - down
        hz[k, 2] = W1 * face + W2 * ((ahead + behind) + (up + down))

    def flags(x, carry):
        for i, c in enumerate(DIRECTIONS[1:]):
            cx, cy, cz = c
            beside = fbuf[x + 1 + cx, 0, 8 + cy:24 + cy, :]
            if cz != 0:
                k = 0 if cz > 0 else 1
                beside = moved(beside, zr[0, k, 0, 8 + cy:24 + cy, :], position(0, x + cx), cz)
            nbuf[x, i] = beside
        return carry

    lax.fori_loop(0, NX, flags, 0)
    sent(0)
    loads[4].wait()

    def stream_plane(s, n, x, faces):
        a = abuf.at[s]
        fl = fbuf[x + 1, 0, OWN, :]

        @functools.cache
        def correction(cx, cy):
            return cor[x + 1 + cx, 8 + cy:24 + cy, :]

        def value(slot, cx, cy):
            stored = a[x + 1 + cx, slot, 8 + cy:24 + cy, :]
            return stored if s == STEPS - 1 else stored - correction(cx, cy)

        own = {c: value(SLOT[c], 0, 0) for c in DIRECTIONS}
        b = {(0, 0, 0): own[(0, 0, 0)]}
        for c in DIRECTIONS[1:]:
            cx, cy, cz = c
            away = value(SLOT[c], cx, cy)
            if cz != 0:
                k = 0 if cz > 0 else 1
                away = moved(away, zr[n, k, 0, 8 + cy:24 + cy, :], position(ZPOP[k].index(c), x + cx), cz)
            b[c] = jnp.where(nbuf[x, DIRECTIONS.index(c) - 1] != 0.0, away, own[tuple(-t for t in c)])
        total = {}
        gap = {}
        for c, o in PAIRS:
            total[c] = b[c] + b[o]
            gap[c] = b[c] - b[o]
        w1, w2 = W1 / TAU, W2 / TAU
        sx, sy, sz = total[(1, 0, 0)], total[(0, 1, 0)], total[(0, 0, 1)]
        pxy, mxy = total[(1, 1, 0)], total[(1, -1, 0)]
        pxz, mxz = total[(1, 0, 1)], total[(1, 0, -1)]
        pyz, myz = total[(0, 1, 1)], total[(0, 1, -1)]
        txy, txz, tyz = pxy + mxy, pxz + mxz, pyz + myz
        m0 = (W0 / TAU) * b[(0, 0, 0)] + w1 * (sx + sy + sz) + w2 * (txy + txz + tyz)
        mxx = w1 * sx + w2 * (txy + txz)
        myy = w1 * sy + w2 * (txy + tyz)
        mzz = w1 * sz + w2 * (txz + tyz)
        hxy, hxz, hyz = w2 * (pxy - mxy), w2 * (pxz - mxz), w2 * (pyz - myz)
        dxp, dxm = gap[(1, 1, 0)], gap[(1, -1, 0)]
        ezp, ezm = gap[(1, 0, 1)], gap[(1, 0, -1)]
        fzp, fzm = gap[(0, 1, 1)], gap[(0, 1, -1)]
        m1x = w1 * gap[(1, 0, 0)] + w2 * ((dxp + dxm) + (ezp + ezm))
        m1y = w1 * gap[(0, 1, 0)] + w2 * ((dxp - dxm) + (fzp + fzm))
        m1z = w1 * gap[(0, 0, 1)] + w2 * ((ezp - ezm) + (fzp - fzm))
        ux, uy, uz_ = ubuf[s, 0, x], ubuf[s, 1, x], ubuf[s, 2, x]
        qx = mxx * ux + hxy * uy + hxz * uz_
        qy = hxy * ux + myy * uy + hyz * uz_
        qz = hxz * ux + hyz * uy + mzz * uz_
        speed = ux * ux + uy * uy + uz_ * uz_
        m3 = 3.0 * m0
        mbar = (3.0 * m1x + 9.0 * qx - ux * m3, 3.0 * m1y + 9.0 * qy - uy * m3, 3.0 * m1z + 9.0 * qz - uz_ * m3)
        fade = jnp.exp(-dbuf[s, x])
        dot = mbar[0] * pbuf[x, 0] + mbar[1] * pbuf[x, 1] + mbar[2] * pbuf[x, 2]
        density_bar = m0 + 1.5 * speed * m0 - 4.5 * (ux * qx + uy * qy + uz_ * qz) - (TAU * fade) * dot
        scale = fl * (TAU * (1.0 - fade))
        packed, packed_v = faces
        for k in range(3):
            force = scale * mbar[k]
            vbuf[s, x + 2, k, OWN, :] = force
            packed_v = pack_v(packed_v, v_position(k, x), force)
        mx, my, mz = mbar
        sums = {(1, 0, 0): mx, (0, 1, 0): my, (0, 0, 1): mz,
                (1, 1, 0): mx + my, (1, -1, 0): mx - my, (1, 0, 1): mx + mz,
                (1, 0, -1): mx - mz, (0, 1, 1): my + mz, (0, 1, -1): my - mz}
        keep = 1.0 - 1.0 / TAU
        populations = {(0, 0, 0): fl * (keep * b[(0, 0, 0)] + density_bar)}
        for c, o in PAIRS:
            populations[c] = fl * (keep * b[c] + (density_bar + sums[c]))
            populations[o] = fl * (keep * b[o] + (density_bar - sums[c]))
        if s > 0:
            packed = store_plane(abuf.at[s - 1], x, populations, packed)
        else:
            for i, c in enumerate(DIRECTIONS):
                obuf[x, i] = populations[c]
        return packed, packed_v

    def force_plane(s, x, carry):
        f = 1 + s
        def phi(cx, cy):
            return fbuf[x + 1 + cx, f, 8 + cy:24 + cy, :]
        pp, pm, mp, mm = phi(1, 1), phi(1, -1), phi(-1, 1), phi(-1, -1)
        xp, xm, yp, ym = phi(1, 0), phi(-1, 0), phi(0, 1), phi(0, -1)
        dx, dy = xp - xm, yp - ym
        t = W1 * phi(0, 0) + W2 * ((xp + xm) + (yp + ym))
        def at(q, values, cz):
            return moved(values, hz[0 if cz > 0 else 1, q], position(f, x), cz)
        pbuf[x, 0] = W1 * dx + W2 * ((pp - mp) + (pm - mm) + (at(0, dx, 1) + at(0, dx, -1)))
        pbuf[x, 1] = W1 * dy + W2 * ((pp - pm) + (mp - mm) + (at(1, dy, 1) + at(1, dy, -1)))
        pbuf[x, 2] = at(2, t, 1) - at(2, t, -1)
        return carry

    def faces_of_v(n, blocks, ring):
        for k in range(2):
            for r, h in blocks:
                face = zr[n, k, 1, r:r + h, :]
                up, down = zr[n, k, 1, r + 1:r + h + 1, :], zr[n, k, 1, r - 1:r + h - 1, :]
                ahead, behind = rolled(face, NZ - 2), rolled(face, 2)
                across = behind - ahead
                along_y = down - up
                around = W1 * face + W2 * ((ahead + behind) + (up + down))
                shares = []
                for depth in range(2 if ring else 1):
                    offset = depth if k == 0 else 1 - depth
                    d = W2 * (back_by(across, offset) + back_by(along_y, offset + 24))
                    shares.append((d, back_by(around, offset + 48)))
                d, t = shares[0]
                uz[k, r:r + h, :] = d - t if k == 0 else d + t
                if not ring:
                    continue
                offset = k
                high, low = back_by(up, 24), back_by(down, 24)
                diagonal = rolled((down + low) + (up - high), 2) - rolled((up + high) + (down - low), NZ - 2)
                far_d, far_t = shares[1]
                zb[k, r:r + h, :] = 2.0 * d + W2 * back_by(diagonal, offset) + (far_d - far_t if k == 0 else far_d + far_t)

    def back_of(s, x, r, h):
        v = vbuf.at[s]
        def at(k, cx, cy):
            return v[x + 2 + cx, k, r + cy:r + cy + h, :]
        d = W2 * ((at(0, -1, 0) - at(0, 1, 0)) + (at(1, 0, -1) - at(1, 0, 1)))
        t = W1 * at(2, 0, 0) + W2 * ((at(2, -1, 0) + at(2, 1, 0)) + (at(2, 0, -1) + at(2, 0, 1)))
        gathered = 2.0 * d + W2 * (
            (at(0, -1, -1) + at(1, -1, -1)) - (at(0, 1, 1) + at(1, 1, 1))
            + (at(0, -1, 1) - at(1, -1, 1)) - (at(0, 1, -1) - at(1, 1, -1)))
        ahead, behind = d + t, d - t
        gathered = (gathered + moved(ahead, uz[1, r:r + h, :], position(0, x), -1)
                    + moved(behind, uz[0, r:r + h, :], position(0, x), 1))
        return gathered, ahead, behind

    def gain(s, x, r, h):
        return fbuf[x + 1, 0, r:r + h, :] * (G - fbuf[x + 1, 1 + s, r:r + h, :])

    def note(s, x, gathered):
        share = (fbuf[x + 1, 0, OWN, :] - 1.0) * gathered
        gbuf[x] = share if s == STEPS - 1 else gbuf[x] + share

    def ring_plane(s, inside, i, carry):
        x = i - 1
        packed = []
        for (r, h), faces in zip(BLOCKS, carry):
            gathered, ahead, behind = back_of(s, x, r, h)
            cor[x + 1, r:r + h, :] = gain(s, x, r, h) * gathered
            if inside and h == NY:
                note(s, x, gathered)
            at = position(0, x)
            mine = lanes_of(gathered) == at
            packed.append((jnp.where(mine, rolled(ahead, at + 1), faces[0]), jnp.where(mine, rolled(behind, at), faces[1])))
        return tuple(packed)

    def correct(s, n):
        faces_of_v(n, BLOCKS, True)
        carry = ((blank, blank), (row, row), (row, row))
        carry = lax.fori_loop(0, 1, functools.partial(ring_plane, s, False), carry, unroll=1)
        carry = lax.fori_loop(1, NX + 1, functools.partial(ring_plane, s, True), carry, unroll=NX)
        carry = lax.fori_loop(NX + 1, NX + 2, functools.partial(ring_plane, s, False), carry, unroll=1)
        for (r, h), faces in zip(BLOCKS, carry):
            for k in range(2):
                fixed_face = zr[0, k, 0, r:r + h, :]
                gamma = fixed_face * (G - back_by(fixed_face, 20 * (1 + s)))
                amount = gamma * (zb[k, r:r + h, :] + faces[k])
                spread = amount
                for j in range(1, 5):
                    spread = jnp.where(lanes_of(amount) >= 20 * j + 1, rolled(amount, 20 * j), spread)
                zr[n, k, 0, r:r + h, :] = zr[n, k, 0, r:r + h, :] - spread

    def last_plane(x, carry):
        gathered, ahead, behind = back_of(0, x, 8, NY)
        note(0, x, gathered)
        amount = gain(0, x, 8, NY) * gathered
        for i in range(19):
            obuf[x, i] = obuf[x, i] - amount
        pltpu.make_async_copy(obuf.at[x], out.at[:, x], out_sem.at[x]).start()
        return carry

    lax.fori_loop(0, NX, functools.partial(force_plane, STEPS - 1), 0)
    for s in reversed(range(STEPS)):
        n = STEPS - s
        a = abuf.at[s]
        receive(n)
        for x in range(NX):
            a[x + 1, SLOT[(1, -1, 0)], 7:8, :] = a[x + 1, COPY, 7:8, :]
        if s < STEPS - 1:
            correct(s + 1, n)
        planes(functools.partial(stream_plane, s, n), n + 1, a=abuf.at[s - 1] if s > 0 else None, v=vbuf.at[s])
        sent(n)
        if s > 0:
            lax.fori_loop(0, NX, functools.partial(force_plane, s - 1), 0)
        else:
            sent(n + 1)
    receive(STEPS + 1)
    faces_of_v(STEPS + 1, BLOCKS[:1], False)
    lax.fori_loop(0, NX, last_plane, 0, unroll=NX)

    last_copy = pltpu.make_async_copy(gbuf, grad, in_sem.at[0])
    last_copy.start()
    for x in range(NX):
        pltpu.make_async_copy(obuf.at[x], out.at[:, x], out_sem.at[x]).wait()
    last_copy.wait()


def solution(mesh):
    sizes = tuple(mesh.shape[a] for a in ("gx", "gy", "gz"))
    f32 = jnp.float32

    def per_device(cotangent, densities, velocities, adhesion, fluid):
        block = (NX, NY, NZ)
        return pl.pallas_call(
            functools.partial(kernel, sizes),
            out_shape=(jax.ShapeDtypeStruct((19,) + block, f32), jax.ShapeDtypeStruct(block, f32)),
            in_specs=[pl.BlockSpec(memory_space=pltpu.HBM)] * 5,
            out_specs=(pl.BlockSpec(memory_space=pltpu.HBM),) * 2,
            scratch_shapes=[
                pltpu.VMEM((19,) + block, f32),
                pltpu.VMEM((STEPS,) + block, f32),
                pltpu.VMEM((STEPS, 3) + block, f32),
                pltpu.VMEM(block, f32),
                pltpu.VMEM(block, jnp.int32),
                pltpu.VMEM((NX + 2, 4, 32, NZ), f32),
                pltpu.VMEM((STEPS, NX + 2, 20, 32, NZ), f32),
                pltpu.VMEM((STEPS, NX + 4, 3, 32, NZ), f32),
                pltpu.VMEM((NX, 3, NY, NZ), f32),
                pltpu.VMEM((NX, 18, NY, NZ), f32),
                pltpu.VMEM((NX, 19, NY, NZ), f32),
                pltpu.VMEM(block, f32),
                pltpu.VMEM((NX + 2, 32, NZ), f32),
                pltpu.VMEM((5, 2, 2, NY, NZ), f32),
                pltpu.VMEM((5, 2, 2, NY, NZ), f32),
                pltpu.VMEM((5, 2, 2, 32, NZ), f32),
                pltpu.VMEM((5, 2, 2, 2, 32, NZ), f32),
                pltpu.VMEM((2, 3, NY, NZ), f32),
                pltpu.VMEM((2, 32, NZ), f32),
                pltpu.VMEM((2, 32, NZ), f32),
                pltpu.VMEM((2, 808, NZ), f32),
                pltpu.SemaphoreType.DMA((5,)),
                pltpu.SemaphoreType.DMA((5,)),
                pltpu.SemaphoreType.DMA((5,)),
                pltpu.SemaphoreType.DMA((NX,)),
            ],
            compiler_params=pltpu.CompilerParams(
                collective_id=0, has_side_effects=True, vmem_limit_bytes=48 * 1024 * 1024),
        )(*[pltpu.with_memory_space_constraint(t, pltpu.HBM) for t in (cotangent, densities, velocities, adhesion, fluid)])

    cells = P("gx", "gy", "gz")
    return jax.shard_map(
        per_device,
        mesh=mesh,
        in_specs=(P(None, "gx", "gy", "gz"), P(None, "gx", "gy", "gz"), P(None, None, "gx", "gy", "gz"), cells, cells),
        out_specs=(P(None, "gx", "gy", "gz"), cells),
        check_vma=False,
    )
```

time: 34.4 us -> 33.4 us (0.971)
  Pallas kernels: 31.9 us -> 31 us
    pallas_call x1, Pallas kernels: 31.9 us -> 31 us  [per_device(): pl.pallas_call(functools.partial(kernel, sizes), out_shape=(jax.ShapeDtyp...]
where the time goes in v3:
time: 33.4 us; the launch traced here: 33.3 us
  Pallas kernels  31 us (93%)
  local copies, waits for them, and re-layouts  1.67 us (5%)
  between operations  0.64 us (2%)
    pallas_call x1, Pallas kernels, per_device(): pl.pallas_call(functools.partial(kernel, sizes), out_shape=(jax.ShapeDtyp...  31 us
    unnamed x2, local copies, waits for them, and re-layouts  1.67 us

profile of v3, /device:TPU:1, one launch (start us, length us, event | category | flops | bytes accessed | tf_op | source)
XLA Modules:
  0.0 33.3 jit_solution(14850988105530859503)
XLA Ops:
  0.6 31.0 %shard_map.68 = (f32[19,8,16,128]{3,2,1,0:T(8,128)S(1)}, f32[8,16,128]{2,1,0:T(8,128)S(1)}) custom-call(f32[19,8,16,128]{3,2,1,0:T(8,128)} %cot.1, f32[3,8,16,128]{3,2,1,0:T(8,128)} %dens.1, f32[3,3,8,16,128]{4,3,2,1,0:T(8,128)} %vel.1, f32[8,16,128]{2,1,0:T(8,128)} %adh.1, s32[8,16,128]{2,1,0:T(8,128)} %flu.1), custom_call_target="tpu_custom_call" | custom-call | tf_op jit(solution)/shard_map/pallas_call | solution.py:542
  31.6 1.0 %copy.9 = f32[19,8,16,128]{3,2,1,0:T(8,128)} copy(f32[19,8,16,128]{3,2,1,0:T(8,128)S(1)} %get-tuple-element.4) | data formatting | bytes 2490368
  32.7 0.6 %copy.10 = f32[8,16,128]{2,1,0:T(8,128)} copy(f32[8,16,128]{2,1,0:T(8,128)S(1)} %get-tuple-element.5) | data formatting | bytes 131072

commit v4 on v3

--- a/solution.py
+++ b/solution.py
@@ -66,9 +66,9 @@
     return values if lanes == 0 else pltpu.roll(values, NZ - lanes, 1)
 
 
-def kernel(sizes, cot, dens, vel, adh, flu, out, grad,
-           cbuf, dbuf, ubuf, adbuf, fibuf, fbuf, abuf, vbuf, pbuf, nbuf, obuf, gbuf, cor,
-           zs, zx, zr, ze, hz, uz, zb, wbuf, send_sem, recv_sem, in_sem, out_sem):
+def kernel(sizes, cot, dens, vel, adh, flu, obuf, amount, gbuf,
+           cbuf, dbuf, ubuf, adbuf, fibuf, fbuf, abuf, vbuf, pbuf, nbuf, cor,
+           zs, zx, zr, ze, hz, uz, zb, wbuf, send_sem, recv_sem, in_sem):
     index = [lax.axis_index(a) for a in ("gx", "gy", "gz")]
     lane = lax.broadcasted_iota(jnp.int32, (NY, NZ), 1)
     lane_row = lax.broadcasted_iota(jnp.int32, (1, NZ), 1)
@@ -185,21 +185,21 @@
     def sent(n):
         await_rows(n, send_sem)
 
-    def planes(plane, n, a=None, v=None, wait=None):
+    def planes(plane, n, a=None, v=None, held=False):
         faces = tuple((blank,) * 2 for part in range(2))
         for x in (0, NX - 2):
             faces = lax.fori_loop(x, x + 2, plane, faces, unroll=2)
         for part in range(2):
             for k in range(2):
                 zx[n, k, part] = faces[part][k]
-        if wait is not None:
-            wait()
-        send(n, a, v, True)
+        if not held:
+            send(n, a, v, True)
         faces = lax.fori_loop(2, NX - 2, plane, faces, unroll=NX - 4)
         for part in range(2):
             for k in range(2):
                 zs[n, k, part] = faces[part][k]
-        send(n, a, v, False)
+        if not held:
+            send(n, a, v, False)
 
     def pack(faces, at, low, high):
         mine = lane == at
@@ -286,11 +286,7 @@
             packed = pack(packed, position(f, x), value, value)
         return packed, faces[1]
 
-    def greeted():
-        pl.semaphore_wait(barrier, sum(here[d].astype(jnp.int32) for d in NEIGHBOURS))
-
-    planes(fixed, 0, wait=greeted)
-
+    planes(fixed, 0, held=True)
     loads[3].wait()
 
     def store_plane(buf, x, populations, packed):
@@ -309,7 +305,11 @@
         packed = store_plane(abuf.at[STEPS - 1], x, {c: fl * cbuf[i, x] for i, c in enumerate(DIRECTIONS)}, faces[0])
         return packed, faces[1]
 
-    planes(masked, 1, a=abuf.at[STEPS - 1])
+    planes(masked, 1, held=True)
+    pl.semaphore_wait(barrier, sum(here[d].astype(jnp.int32) for d in NEIGHBOURS))
+    for n in range(2):
+        for along_x in (True, False):
+            send(n, abuf.at[STEPS - 1], None, along_x)
 
     receive(0)
     for k in range(2):
@@ -330,7 +330,7 @@
             nbuf[x, i] = beside
         return carry
 
-    lax.fori_loop(0, NX, flags, 0)
+    lax.fori_loop(0, NX, flags, 0, unroll=NX)
     sent(0)
     loads[4].wait()
 
@@ -501,13 +501,10 @@
     def last_plane(x, carry):
         gathered, ahead, behind = back_of(0, x, 8, NY)
         note(0, x, gathered)
-        amount = gain(0, x, 8, NY) * gathered
-        for i in range(19):
-            obuf[x, i] = obuf[x, i] - amount
-        pltpu.make_async_copy(obuf.at[x], out.at[:, x], out_sem.at[x]).start()
+        amount[x] = gain(0, x, 8, NY) * gathered
         return carry
 
-    lax.fori_loop(0, NX, functools.partial(force_plane, STEPS - 1), 0)
+    lax.fori_loop(0, NX, functools.partial(force_plane, STEPS - 1), 0, unroll=NX)
     for s in reversed(range(STEPS)):
         n = STEPS - s
         a = abuf.at[s]
@@ -526,11 +523,18 @@
     faces_of_v(STEPS + 1, BLOCKS[:1], False)
     lax.fori_loop(0, NX, last_plane, 0, unroll=NX)
 
-    last_copy = pltpu.make_async_copy(gbuf, grad, in_sem.at[0])
-    last_copy.start()
+
+def finish(part, amount, share, out, grad, obuf, sems):
+    copies = [pltpu.make_async_copy(share, grad, sems.at[NX])]
+    copies[0].start()
     for x in range(NX):
-        pltpu.make_async_copy(obuf.at[x], out.at[:, x], out_sem.at[x]).wait()
-    last_copy.wait()
+        back = amount[x]
+        for i in range(19):
+            obuf[x, i] = part[x, i] - back
+        copies.append(pltpu.make_async_copy(obuf.at[x], out.at[:, x], sems.at[x]))
+        copies[-1].start()
+    for copy in copies:
+        copy.wait()
 
 
 def solution(mesh):
@@ -539,11 +543,13 @@
 
     def per_device(cotangent, densities, velocities, adhesion, fluid):
         block = (NX, NY, NZ)
-        return pl.pallas_call(
+        in_vmem = pl.BlockSpec(memory_space=pltpu.VMEM)
+        results = pl.pallas_call(
             functools.partial(kernel, sizes),
-            out_shape=(jax.ShapeDtypeStruct((19,) + block, f32), jax.ShapeDtypeStruct(block, f32)),
+            out_shape=(
+                jax.ShapeDtypeStruct((NX, 19, NY, NZ), f32), jax.ShapeDtypeStruct(block, f32), jax.ShapeDtypeStruct(block, f32)),
             in_specs=[pl.BlockSpec(memory_space=pltpu.HBM)] * 5,
-            out_specs=(pl.BlockSpec(memory_space=pltpu.HBM),) * 2,
+            out_specs=(in_vmem,) * 3,
             scratch_shapes=[
                 pltpu.VMEM((19,) + block, f32),
                 pltpu.VMEM((STEPS,) + block, f32),
@@ -555,8 +561,6 @@
                 pltpu.VMEM((STEPS, NX + 4, 3, 32, NZ), f32),
                 pltpu.VMEM((NX, 3, NY, NZ), f32),
                 pltpu.VMEM((NX, 18, NY, NZ), f32),
-                pltpu.VMEM((NX, 19, NY, NZ), f32),
-                pltpu.VMEM(block, f32),
                 pltpu.VMEM((NX + 2, 32, NZ), f32),
                 pltpu.VMEM((5, 2, 2, NY, NZ), f32),
                 pltpu.VMEM((5, 2, 2, NY, NZ), f32),
@@ -569,11 +573,18 @@
                 pltpu.SemaphoreType.DMA((5,)),
                 pltpu.SemaphoreType.DMA((5,)),
                 pltpu.SemaphoreType.DMA((5,)),
-                pltpu.SemaphoreType.DMA((NX,)),
             ],
             compiler_params=pltpu.CompilerParams(
                 collective_id=0, has_side_effects=True, vmem_limit_bytes=48 * 1024 * 1024),
         )(*[pltpu.with_memory_space_constraint(t, pltpu.HBM) for t in (cotangent, densities, velocities, adhesion, fluid)])
+        return pl.pallas_call(
+            finish,
+            out_shape=(jax.ShapeDtypeStruct((19,) + block, f32), jax.ShapeDtypeStruct(block, f32)),
+            in_specs=[in_vmem] * 3,
+            out_specs=(pl.BlockSpec(memory_space=pltpu.HBM),) * 2,
+            scratch_shapes=[pltpu.VMEM((NX, 19, NY, NZ), f32), pltpu.SemaphoreType.DMA((NX + 1,))],
+            compiler_params=pltpu.CompilerParams(vmem_limit_bytes=8 * 1024 * 1024),
+        )(*results)
 
     cells = P("gx", "gy", "gz")
     return jax.shard_map(

time: 33.4 us -> 31.1 us (0.931)
  local copies, waits for them, and re-layouts: 1.67 us -> 0 us
  Pallas kernels: 31 us -> 30.3 us
    pallas_call x1, Pallas kernels: 31 us -> 29.2 us  [per_device(): pl.pallas_call(functools.partial(kernel, sizes), out_shape=(jax.ShapeDtyp...]
    unnamed x2 -> x0, local copies, waits for them, and re-layouts: 1.67 us -> none
    pallas_call x0 -> x1, Pallas kernels: none -> 1.12 us  [per_device(): pl.pallas_call(finish, out_shape=(jax.ShapeDtypeStruct((19,) + block, f32...]
where the time goes in v4:
time: 31.1 us; the launch traced here: 30.9 us
  Pallas kernels  30.3 us (97%)
  between operations  0.64 us (2%)
    pallas_call x1, Pallas kernels, per_device(): pl.pallas_call(functools.partial(kernel, sizes), out_shape=(jax.ShapeDtyp...  29.2 us
    pallas_call x1, Pallas kernels, per_device(): pl.pallas_call(finish, out_shape=(jax.ShapeDtypeStruct((19,) + block, f32...  1.12 us

profile of v4, /device:TPU:1, one launch (start us, length us, event | category | flops | bytes accessed | tf_op | source)
XLA Modules:
  0.0 30.9 jit_solution(3198989216323890665)
XLA Ops:
  0.6 29.2 %shard_map.68 = (f32[8,19,16,128]{3,2,1,0:T(8,128)S(1)}, f32[8,16,128]{2,1,0:T(8,128)S(1)}, f32[8,16,128]{2,1,0:T(8,128)S(1)}) custom-call(f32[19,8,16,128]{3,2,1,0:T(8,128)} %cot.1, f32[3,8,16,128]{3,2,1,0:T(8,128)} %dens.1, f32[3,3,8,16,128]{4,3,2,1,0:T(8,128)} %vel.1, f32[8,16,128]{2,1,0:T(8,128)} %adh.1, s32[8,16,128]{2,1,0:T(8,128)} %flu.1), custom_call_target="tpu_custom_call" | custom-call | tf_op jit(solution)/shard_map/pallas_call | solution.py:547
  29.8 1.1 %shard_map.69 = (f32[19,8,16,128]{3,2,1,0:T(8,128)}, f32[8,16,128]{2,1,0:T(8,128)}) custom-call(f32[8,19,16,128]{3,2,1,0:T(8,128)S(1)} %get-tuple-element.5.part, f32[8,16,128]{2,1,0:T(8,128)S(1)} %get-tuple-element.6.amount, f32[8,16,128]{2,1,0:T(8,128)S(1)} %get-tuple-element.7.share), custom_call_target="tpu_custom_call" | custom-call | tf_op jit(solution)/shard_map/pallas_call | solution.py:580

commit v5 on v4

--- a/solution.py
+++ b/solution.py
@@ -38,7 +38,7 @@
 PAIRS = tuple((c, tuple(-t for t in c)) for c in DIRECTIONS[1::2])
 NEIGHBOURS = sorted(
     (d for d in itertools.product((-1, 0, 1), repeat=3) if any(d)),
-    key=lambda d: (-abs(d[0]), d[2] != 0, sum(map(abs, d))))
+    key=lambda d: (-abs(d[0]), -sum(map(abs, d)), d[2] != 0))
 BLOCKS = ((8, NY), (7, 1), (24, 1))
 KINDS = ("f", "a", "m", "m", "v")
 ROWS = {
@@ -147,22 +147,27 @@
             def _():
                 for source, target in pairs:
                     pltpu.make_async_remote_copy(
-                        src_ref=source, dst_ref=target, send_sem=send_sem.at[n], recv_sem=recv_sem.at[n],
+                        src_ref=source, dst_ref=target, send_sem=send_sem.at[n], recv_sem=recv_sem.at[n, abs(d[0])],
                         device_id=device(d), device_id_type=MESH).start()
 
-    def await_rows(n, sem):
+    def await_rows(n, sem, wanted):
         for counts in itertools.product((1, 2), repeat=3):
             rows = 0
             for axes, size in ROWS[KINDS[n]].items():
+                if not wanted(axes):
+                    continue
                 for t, used in zip(counts, axes):
                     size = size * t if used else size
                 rows += size
             @pl.when(functools.reduce(jnp.logical_and, [t == c for t, c in zip(along, counts)]))
             def _():
-                pltpu.make_async_copy(wbuf.at[0, pl.ds(0, rows)], wbuf.at[1, pl.ds(0, rows)], sem.at[n]).wait()
-
-    def receive(n):
-        await_rows(n, recv_sem)
+                pltpu.make_async_copy(wbuf.at[0, pl.ds(0, rows)], wbuf.at[1, pl.ds(0, rows)], sem).wait()
+
+    def receive_inner(n):
+        await_rows(n, recv_sem.at[n, 0], lambda axes: axes[0] == 0)
+
+    def receive_ends(n):
+        await_rows(n, recv_sem.at[n, 1], lambda axes: axes[0] == 1)
         kind = KINDS[n]
         ranges = []
         if kind != "v":
@@ -183,7 +188,7 @@
                     zr[n, k, part, r:r + 16, :] = face
 
     def sent(n):
-        await_rows(n, send_sem)
+        await_rows(n, send_sem.at[n], lambda axes: True)
 
     def planes(plane, n, a=None, v=None, held=False):
         faces = tuple((blank,) * 2 for part in range(2))
@@ -214,6 +219,12 @@
         mine = jnp.logical_or(lane == at, lane == at + 1)
         return jnp.where(mine, rolled(value, at), faces[0]), jnp.where(mine, rolled(value, at + 2), faces[1])
 
+    def inner_planes(plane):
+        lax.fori_loop(1, NX - 1, plane, 0, unroll=NX - 2)
+
+    def end_planes(plane):
+        lax.fori_loop(0, 2, lambda i, carry: plane((NX - 1) * i, carry), 0, unroll=2)
+
     def moved(values, packed, at, cz):
         if cz > 0:
             return jnp.where(lanes_of(values) == NZ - 1, rolled(packed, NZ - 1 - at), rolled(values, NZ - 1))
@@ -226,7 +237,8 @@
     for load in loads:
         load.start()
     barrier = pltpu.get_barrier_semaphore()
-    for d in NEIGHBOURS:
+    greeted = [d for d in NEIGHBOURS if 0 in d]
+    for d in greeted:
         @pl.when(here[d])
         def _():
             pl.semaphore_signal(barrier, inc=1, device_id=device(d), device_id_type=MESH)
@@ -306,19 +318,19 @@
         return packed, faces[1]
 
     planes(masked, 1, held=True)
-    pl.semaphore_wait(barrier, sum(here[d].astype(jnp.int32) for d in NEIGHBOURS))
+    pl.semaphore_wait(barrier, sum(here[d].astype(jnp.int32) for d in greeted))
     for n in range(2):
         for along_x in (True, False):
             send(n, abuf.at[STEPS - 1], None, along_x)
 
-    receive(0)
-    for k in range(2):
-        face = zr[0, k, 0, OWN, :]
-        up, down = zr[0, k, 0, 9:25, :], zr[0, k, 0, 7:23, :]
-        ahead, behind = rolled(face, NZ - 2), rolled(face, 2)
-        hz[k, 0] = ahead - behind
-        hz[k, 1] = up - down
-        hz[k, 2] = W1 * face + W2 * ((ahead + behind) + (up + down))
+    def faces_of_phi():
+        for k in range(2):
+            face = zr[0, k, 0, OWN, :]
+            up, down = zr[0, k, 0, 9:25, :], zr[0, k, 0, 7:23, :]
+            ahead, behind = rolled(face, NZ - 2), rolled(face, 2)
+            hz[k, 0] = ahead - behind
+            hz[k, 1] = up - down
+            hz[k, 2] = W1 * face + W2 * ((ahead + behind) + (up + down))
 
     def flags(x, carry):
         for i, c in enumerate(DIRECTIONS[1:]):
@@ -329,10 +341,6 @@
                 beside = moved(beside, zr[0, k, 0, 8 + cy:24 + cy, :], position(0, x + cx), cz)
             nbuf[x, i] = beside
         return carry
-
-    lax.fori_loop(0, NX, flags, 0, unroll=NX)
-    sent(0)
-    loads[4].wait()
 
     def stream_plane(s, n, x, faces):
         a = abuf.at[s]
@@ -483,11 +491,14 @@
         return tuple(packed)
 
     def correct(s, n):
+        carry = ((blank, blank), (row, row), (row, row))
+        receive_inner(n)
+        faces_of_v(n, BLOCKS, False)
+        carry = lax.fori_loop(2, NX, functools.partial(ring_plane, s, True), carry, unroll=NX - 2)
+        receive_ends(n)
         faces_of_v(n, BLOCKS, True)
-        carry = ((blank, blank), (row, row), (row, row))
-        carry = lax.fori_loop(0, 1, functools.partial(ring_plane, s, False), carry, unroll=1)
-        carry = lax.fori_loop(1, NX + 1, functools.partial(ring_plane, s, True), carry, unroll=NX)
-        carry = lax.fori_loop(NX + 1, NX + 2, functools.partial(ring_plane, s, False), carry, unroll=1)
+        for i, inside in ((0, False), (1, True), (NX, True), (NX + 1, False)):
+            carry = lax.fori_loop(i, i + 1, functools.partial(ring_plane, s, inside), carry, unroll=1)
         for (r, h), faces in zip(BLOCKS, carry):
             for k in range(2):
                 fixed_face = zr[0, k, 0, r:r + h, :]
@@ -504,24 +515,40 @@
         amount[x] = gain(0, x, 8, NY) * gathered
         return carry
 
-    lax.fori_loop(0, NX, functools.partial(force_plane, STEPS - 1), 0, unroll=NX)
+    def flags_and_force(x, carry):
+        flags(x, carry)
+        return force_plane(STEPS - 1, x, carry)
+
+    receive_inner(0)
+    faces_of_phi()
+    inner_planes(flags_and_force)
+    receive_ends(0)
+    faces_of_phi()
+    end_planes(flags_and_force)
+    sent(0)
+    loads[4].wait()
     for s in reversed(range(STEPS)):
         n = STEPS - s
         a = abuf.at[s]
-        receive(n)
+        if s < STEPS - 1:
+            correct(s + 1, n)
+        else:
+            receive_inner(n)
+            receive_ends(n)
         for x in range(NX):
             a[x + 1, SLOT[(1, -1, 0)], 7:8, :] = a[x + 1, COPY, 7:8, :]
-        if s < STEPS - 1:
-            correct(s + 1, n)
         planes(functools.partial(stream_plane, s, n), n + 1, a=abuf.at[s - 1] if s > 0 else None, v=vbuf.at[s])
         sent(n)
         if s > 0:
             lax.fori_loop(0, NX, functools.partial(force_plane, s - 1), 0)
         else:
             sent(n + 1)
-    receive(STEPS + 1)
+    receive_inner(STEPS + 1)
     faces_of_v(STEPS + 1, BLOCKS[:1], False)
-    lax.fori_loop(0, NX, last_plane, 0, unroll=NX)
+    inner_planes(last_plane)
+    receive_ends(STEPS + 1)
+    faces_of_v(STEPS + 1, BLOCKS[:1], False)
+    end_planes(last_plane)
 
 
 def finish(part, amount, share, out, grad, obuf, sems):
@@ -571,7 +598,7 @@
                 pltpu.VMEM((2, 32, NZ), f32),
                 pltpu.VMEM((2, 808, NZ), f32),
                 pltpu.SemaphoreType.DMA((5,)),
-                pltpu.SemaphoreType.DMA((5,)),
+                pltpu.SemaphoreType.DMA((5, 2)),
                 pltpu.SemaphoreType.DMA((5,)),
             ],
             compiler_params=pltpu.CompilerParams(

time: 31.1 us -> 29.9 us (0.961)
  Pallas kernels: 30.3 us -> 29.1 us
    pallas_call x1, Pallas kernels: 29.2 us -> 28 us  [per_device(): pl.pallas_call(functools.partial(kernel, sizes), out_shape=(jax.ShapeDtyp...]
where the time goes in v5:
time: 29.9 us; the launch traced here: 29.7 us
  Pallas kernels  29.1 us (97%)
  between operations  0.64 us (2%)
    pallas_call x1, Pallas kernels, per_device(): pl.pallas_call(functools.partial(kernel, sizes), out_shape=(jax.ShapeDtyp...  28 us
    pallas_call x1, Pallas kernels, per_device(): pl.pallas_call(finish, out_shape=(jax.ShapeDtypeStruct((19,) + block, f32...  1.12 us

profile of v5, /device:TPU:1, one launch (start us, length us, event | category | flops | bytes accessed | tf_op | source)
XLA Modules:
  0.0 29.7 jit_solution(17753875532535432888)
XLA Ops:
  0.6 28.0 %shard_map.68 = (f32[8,19,16,128]{3,2,1,0:T(8,128)S(1)}, f32[8,16,128]{2,1,0:T(8,128)S(1)}, f32[8,16,128]{2,1,0:T(8,128)S(1)}) custom-call(f32[19,8,16,128]{3,2,1,0:T(8,128)} %cot.1, f32[3,8,16,128]{3,2,1,0:T(8,128)} %dens.1, f32[3,3,8,16,128]{4,3,2,1,0:T(8,128)} %vel.1, f32[8,16,128]{2,1,0:T(8,128)} %adh.1, s32[8,16,128]{2,1,0:T(8,128)} %flu.1), custom_call_target="tpu_custom_call" | custom-call | tf_op jit(solution)/shard_map/pallas_call | solution.py:574
  28.6 1.1 %shard_map.69 = (f32[19,8,16,128]{3,2,1,0:T(8,128)}, f32[8,16,128]{2,1,0:T(8,128)}) custom-call(f32[8,19,16,128]{3,2,1,0:T(8,128)S(1)} %get-tuple-element.5.part, f32[8,16,128]{2,1,0:T(8,128)S(1)} %get-tuple-element.6.amount, f32[8,16,128]{2,1,0:T(8,128)S(1)} %get-tuple-element.7.share), custom_call_target="tpu_custom_call" | custom-call | tf_op jit(solution)/shard_map/pallas_call | solution.py:607

commit v6 on v5

--- a/solution.py
+++ b/solution.py
@@ -31,9 +31,10 @@
 )
 SLOT = {c: k for k, c in enumerate(SLOTS) if c is not None}
 COPY = 16
+SHARED = 74
 ZPOP = (
-    ((0, 0, 1), (1, 0, 1), (-1, 0, 1), (0, 1, 1), (0, -1, 1)),
-    ((0, 0, -1), (1, 0, -1), (-1, 0, -1), (0, 1, -1), (0, -1, -1)),
+    ((0, 0, 1), (0, 1, 1), (0, -1, 1), (1, 0, 1), (-1, 0, 1)),
+    ((0, 0, -1), (0, 1, -1), (0, -1, -1), (1, 0, -1), (-1, 0, -1)),
 )
 PAIRS = tuple((c, tuple(-t for t in c)) for c in DIRECTIONS[1::2])
 NEIGHBOURS = sorted(
@@ -44,14 +45,14 @@
 ROWS = {
     "f": {(1, 0, 0): 64, (0, 1, 0): 32, (0, 0, 1): 16, (1, 1, 0): 4, (1, 0, 1): 16, (0, 1, 1): 1},
     "a": {(1, 0, 0): 80, (0, 1, 0): 40, (0, 0, 1): 16, (1, 1, 0): 1, (1, 0, 1): 16, (0, 1, 1): 1},
-    "m": {(1, 0, 0): 176, (0, 1, 0): 88, (0, 0, 1): 32, (1, 1, 0): 13, (1, 0, 1): 32, (0, 1, 1): 4, (1, 1, 1): 2},
+    "m": {(1, 0, 0): 176, (0, 1, 0): 88, (0, 0, 1): 32, (1, 1, 0): 13, (1, 0, 1): 16, (0, 1, 1): 4, (1, 1, 1): 2},
     "v": {(1, 0, 0): 48, (0, 1, 0): 24, (0, 0, 1): 16, (1, 1, 0): 3, (1, 0, 1): 16, (0, 1, 1): 1},
 }
 OWN = pl.ds(8, NY)
 
 
 def position(field, x):
-    return 4 + 20 * field + 2 * x
+    return 4 + 24 * field + 2 * x
 
 
 def v_position(k, x):
@@ -134,7 +135,7 @@
             ys = (pl.ds(0, NY), OWN)
         if dx == 0:
             return [(zs.at[n, k, parts, ys[0]], zr.at[n, k, parts, ys[1]])]
-        if dy != 0:
+        if kind == "m":
             parts = pl.ds(1, 1)
         return [(zx.at[n, k, parts, ys[0]], ze.at[n, k, e, parts, ys[1]])]
 
@@ -171,8 +172,8 @@
         kind = KINDS[n]
         ranges = []
         if kind != "v":
-            fields = 4 if kind == "f" else 5
-            ranges.append((0, [position(f, NX) for f in range(fields)], [position(f, -1) for f in range(fields)], 1))
+            fields = range(4) if kind == "f" else (3, 4)
+            ranges.append((0, [position(f, NX) for f in fields], [position(f, -1) for f in fields], 1))
         if kind in "mv":
             ranges.append((1, [v_position(f, NX) for f in range(3)], [v_position(f, -2) for f in range(3)], 4))
         for part, rights, lefts, width in ranges:
@@ -180,11 +181,12 @@
             right = functools.reduce(jnp.logical_or, [inside(at) for at in rights])
             left = functools.reduce(jnp.logical_or, [inside(at) for at in lefts])
             rows = (0, 16) if part == 1 else (8,)
+            held = 1 if kind == "m" else part
             for k in range(2):
                 for r in rows:
                     face = zr[n, k, part, r:r + 16, :]
-                    face = jnp.where(right, rolled(ze[n, k, 0, part, r:r + 16, :], 16), face)
-                    face = jnp.where(left, rolled(ze[n, k, 1, part, r:r + 16, :], NZ - 16), face)
+                    face = jnp.where(right, rolled(ze[n, k, 0, held, r:r + 16, :], 16), face)
+                    face = jnp.where(left, rolled(ze[n, k, 1, held, r:r + 16, :], NZ - 16), face)
                     zr[n, k, part, r:r + 16, :] = face
 
     def sent(n):
@@ -192,14 +194,18 @@
 
     def planes(plane, n, a=None, v=None, held=False):
         faces = tuple((blank,) * 2 for part in range(2))
-        for x in (0, NX - 2):
-            faces = lax.fori_loop(x, x + 2, plane, faces, unroll=2)
+        ends = 2 if KINDS[n] == "m" else 1
+        for x in (0, NX - ends):
+            faces = lax.fori_loop(x, x + ends, plane, faces, unroll=ends)
         for part in range(2):
             for k in range(2):
-                zx[n, k, part] = faces[part][k]
+                face = faces[part][k]
+                if KINDS[n] == "m" and part == 1:
+                    face = jnp.where(lane >= SHARED, faces[0][k], face)
+                zx[n, k, part] = face
         if not held:
             send(n, a, v, True)
-        faces = lax.fori_loop(2, NX - 2, plane, faces, unroll=NX - 4)
+        faces = lax.fori_loop(ends, NX - ends, plane, faces, unroll=NX - 2 * ends)
         for part in range(2):
             for k in range(2):
                 zs[n, k, part] = faces[part][k]
@@ -342,6 +348,18 @@
             nbuf[x, i] = beside
         return carry
 
+    def leaving(fl, b, density_bar, mbar):
+        mx, my, mz = mbar
+        sums = {(1, 0, 0): mx, (0, 1, 0): my, (0, 0, 1): mz,
+                (1, 1, 0): mx + my, (1, -1, 0): mx - my, (1, 0, 1): mx + mz,
+                (1, 0, -1): mx - mz, (0, 1, 1): my + mz, (0, 1, -1): my - mz}
+        keep = 1.0 - 1.0 / TAU
+        populations = {(0, 0, 0): fl * (keep * b[(0, 0, 0)] + density_bar)}
+        for c, o in PAIRS:
+            populations[c] = fl * (keep * b[c] + (density_bar + sums[c]))
+            populations[o] = fl * (keep * b[o] + (density_bar - sums[c]))
+        return populations
+
     def stream_plane(s, n, x, faces):
         a = abuf.at[s]
         fl = fbuf[x + 1, 0, OWN, :]
@@ -401,21 +419,21 @@
             force = scale * mbar[k]
             vbuf[s, x + 2, k, OWN, :] = force
             packed_v = pack_v(packed_v, v_position(k, x), force)
-        mx, my, mz = mbar
-        sums = {(1, 0, 0): mx, (0, 1, 0): my, (0, 0, 1): mz,
-                (1, 1, 0): mx + my, (1, -1, 0): mx - my, (1, 0, 1): mx + mz,
-                (1, 0, -1): mx - mz, (0, 1, 1): my + mz, (0, 1, -1): my - mz}
-        keep = 1.0 - 1.0 / TAU
-        populations = {(0, 0, 0): fl * (keep * b[(0, 0, 0)] + density_bar)}
-        for c, o in PAIRS:
-            populations[c] = fl * (keep * b[c] + (density_bar + sums[c]))
-            populations[o] = fl * (keep * b[o] + (density_bar - sums[c]))
         if s > 0:
-            packed = store_plane(abuf.at[s - 1], x, populations, packed)
+            packed = store_plane(abuf.at[s - 1], x, leaving(fl, b, density_bar, mbar), packed)
         else:
             for i, c in enumerate(DIRECTIONS):
-                obuf[x, i] = populations[c]
+                obuf[x, i] = b[c]
+            for k, kept in enumerate((density_bar,) + mbar):
+                cbuf[k, x] = kept
         return packed, packed_v
+
+    def leave_plane(x, carry):
+        populations = leaving(
+            fbuf[x + 1, 0, OWN, :], {c: obuf[x, i] for i, c in enumerate(DIRECTIONS)}, cbuf[0, x], [cbuf[1 + k, x] for k in range(3)])
+        for i, c in enumerate(DIRECTIONS):
+            obuf[x, i] = populations[c]
+        return carry
 
     def force_plane(s, x, carry):
         f = 1 + s
@@ -502,11 +520,11 @@
         for (r, h), faces in zip(BLOCKS, carry):
             for k in range(2):
                 fixed_face = zr[0, k, 0, r:r + h, :]
-                gamma = fixed_face * (G - back_by(fixed_face, 20 * (1 + s)))
+                gamma = fixed_face * (G - back_by(fixed_face, 24 * (1 + s)))
                 amount = gamma * (zb[k, r:r + h, :] + faces[k])
                 spread = amount
                 for j in range(1, 5):
-                    spread = jnp.where(lanes_of(amount) >= 20 * j + 1, rolled(amount, 20 * j), spread)
+                    spread = jnp.where(lanes_of(amount) >= 24 * j + 1, rolled(amount, 24 * j), spread)
                 zr[n, k, 0, r:r + h, :] = zr[n, k, 0, r:r + h, :] - spread
 
     def last_plane(x, carry):
@@ -542,6 +560,7 @@
         if s > 0:
             lax.fori_loop(0, NX, functools.partial(force_plane, s - 1), 0)
         else:
+            lax.fori_loop(0, NX, leave_plane, 0, unroll=2)
             sent(n + 1)
     receive_inner(STEPS + 1)
     faces_of_v(STEPS + 1, BLOCKS[:1], False)

time: 29.9 us -> 29.2 us (0.977)
  Pallas kernels: 29.1 us -> 28.5 us
    pallas_call x1, Pallas kernels: 28 us -> 27.3 us  [per_device(): pl.pallas_call(functools.partial(kernel, sizes), out_shape=(jax.ShapeDtyp...]
where the time goes in v6:
time: 29.2 us; the launch traced here: 29.1 us
  Pallas kernels  28.5 us (98%)
  between operations  0.64 us (2%)
    pallas_call x1, Pallas kernels, per_device(): pl.pallas_call(functools.partial(kernel, sizes), out_shape=(jax.ShapeDtyp...  27.3 us
    pallas_call x1, Pallas kernels, per_device(): pl.pallas_call(finish, out_shape=(jax.ShapeDtypeStruct((19,) + block, f32...  1.12 us

profile of v6, /device:TPU:1, one launch (start us, length us, event | category | flops | bytes accessed | tf_op | source)
XLA Modules:
  0.0 29.1 jit_solution(3604091036268329488)
XLA Ops:
  0.6 27.3 %shard_map.68 = (f32[8,19,16,128]{3,2,1,0:T(8,128)S(1)}, f32[8,16,128]{2,1,0:T(8,128)S(1)}, f32[8,16,128]{2,1,0:T(8,128)S(1)}) custom-call(f32[19,8,16,128]{3,2,1,0:T(8,128)} %cot.1, f32[3,8,16,128]{3,2,1,0:T(8,128)} %dens.1, f32[3,3,8,16,128]{4,3,2,1,0:T(8,128)} %vel.1, f32[8,16,128]{2,1,0:T(8,128)} %adh.1, s32[8,16,128]{2,1,0:T(8,128)} %flu.1), custom_call_target="tpu_custom_call" | custom-call | tf_op jit(solution)/shard_map/pallas_call | solution.py:593
  28.0 1.1 %shard_map.69 = (f32[19,8,16,128]{3,2,1,0:T(8,128)}, f32[8,16,128]{2,1,0:T(8,128)}) custom-call(f32[8,19,16,128]{3,2,1,0:T(8,128)S(1)} %get-tuple-element.5.part, f32[8,16,128]{2,1,0:T(8,128)S(1)} %get-tuple-element.6.amount, f32[8,16,128]{2,1,0:T(8,128)S(1)} %get-tuple-element.7.share), custom_call_target="tpu_custom_call" | custom-call | tf_op jit(solution)/shard_map/pallas_call | solution.py:626

commit v7 on v6

--- a/solution.py
+++ b/solution.py
@@ -152,7 +152,8 @@
                         device_id=device(d), device_id_type=MESH).start()
 
     def await_rows(n, sem, wanted):
-        for counts in itertools.product((1, 2), repeat=3):
+        used_axes = [any(axes[i] for axes in ROWS[KINDS[n]] if wanted(axes)) for i in range(3)]
+        for counts in itertools.product(*((1, 2) if used else (0,) for used in used_axes)):
             rows = 0
             for axes, size in ROWS[KINDS[n]].items():
                 if not wanted(axes):
@@ -160,7 +161,7 @@
                 for t, used in zip(counts, axes):
                     size = size * t if used else size
                 rows += size
-            @pl.when(functools.reduce(jnp.logical_and, [t == c for t, c in zip(along, counts)]))
+            @pl.when(functools.reduce(jnp.logical_and, [t == c for t, c in zip(along, counts) if c]))
             def _():
                 pltpu.make_async_copy(wbuf.at[0, pl.ds(0, rows)], wbuf.at[1, pl.ds(0, rows)], sem).wait()
 
@@ -236,18 +237,18 @@
             return jnp.where(lanes_of(values) == NZ - 1, rolled(packed, NZ - 1 - at), rolled(values, NZ - 1))
         return jnp.where(lanes_of(values) == 0, rolled(packed, NZ - at), rolled(values, 1))
 
+    barrier = pltpu.get_barrier_semaphore()
+    greeted = [d for d in NEIGHBOURS if 0 in d]
+    for d in greeted:
+        @pl.when(here[d])
+        def _():
+            pl.semaphore_signal(barrier, inc=1, device_id=device(d), device_id_type=MESH)
     loads = [
         pltpu.make_async_copy(source, target, in_sem.at[k])
         for k, (source, target) in enumerate(((flu, fibuf), (adh, adbuf), (dens, dbuf), (cot, cbuf), (vel, ubuf)))
     ]
     for load in loads:
         load.start()
-    barrier = pltpu.get_barrier_semaphore()
-    greeted = [d for d in NEIGHBOURS if 0 in d]
-    for d in greeted:
-        @pl.when(here[d])
-        def _():
-            pl.semaphore_signal(barrier, inc=1, device_id=device(d), device_id_type=MESH)
     blank = jnp.zeros((NY, NZ), jnp.float32)
     row = jnp.zeros((1, NZ), jnp.float32)
     two_rows = jnp.zeros((2, NZ), jnp.float32)
@@ -558,9 +559,9 @@
         planes(functools.partial(stream_plane, s, n), n + 1, a=abuf.at[s - 1] if s > 0 else None, v=vbuf.at[s])
         sent(n)
         if s > 0:
-            lax.fori_loop(0, NX, functools.partial(force_plane, s - 1), 0)
+            lax.fori_loop(0, NX, functools.partial(force_plane, s - 1), 0, unroll=4)
         else:
-            lax.fori_loop(0, NX, leave_plane, 0, unroll=2)
+            lax.fori_loop(0, NX, leave_plane, 0, unroll=4)
             sent(n + 1)
     receive_inner(STEPS + 1)
     faces_of_v(STEPS + 1, BLOCKS[:1], False)

time: 29.2 us -> 29.2 us (level)
  no operation moved by 1% of the time
where the time goes in v7:
time: 29.2 us; the launch traced here: 29.1 us
  Pallas kernels  28.5 us (98%)
  between operations  0.64 us (2%)
    pallas_call x1, Pallas kernels, per_device(): pl.pallas_call(functools.partial(kernel, sizes), out_shape=(jax.ShapeDtyp...  27.3 us
    pallas_call x1, Pallas kernels, per_device(): pl.pallas_call(finish, out_shape=(jax.ShapeDtypeStruct((19,) + block, f32...  1.12 us

profile of v7, /device:TPU:1, one launch (start us, length us, event | category | flops | bytes accessed | tf_op | source)
XLA Modules:
  0.0 29.1 jit_solution(11820334606661560713)
XLA Ops:
  0.6 27.3 %shard_map.68 = (f32[8,19,16,128]{3,2,1,0:T(8,128)S(1)}, f32[8,16,128]{2,1,0:T(8,128)S(1)}, f32[8,16,128]{2,1,0:T(8,128)S(1)}) custom-call(f32[19,8,16,128]{3,2,1,0:T(8,128)} %cot.1, f32[3,8,16,128]{3,2,1,0:T(8,128)} %dens.1, f32[3,3,8,16,128]{4,3,2,1,0:T(8,128)} %vel.1, f32[8,16,128]{2,1,0:T(8,128)} %adh.1, s32[8,16,128]{2,1,0:T(8,128)} %flu.1), custom_call_target="tpu_custom_call" | custom-call | tf_op jit(solution)/shard_map/pallas_call | solution.py:594
  28.0 1.1 %shard_map.69 = (f32[19,8,16,128]{3,2,1,0:T(8,128)}, f32[8,16,128]{2,1,0:T(8,128)}) custom-call(f32[8,19,16,128]{3,2,1,0:T(8,128)S(1)} %get-tuple-element.5.part, f32[8,16,128]{2,1,0:T(8,128)S(1)} %get-tuple-element.6.amount, f32[8,16,128]{2,1,0:T(8,128)S(1)} %get-tuple-element.7.share), custom_call_target="tpu_custom_call" | custom-call | tf_op jit(solution)/shard_map/pallas_call | solution.py:627
